TPU v7x, 256 devices: a whole 4x4x8 slice. The times are simulated.
256 devices in a mesh: view: 16 (over y, x), scene: 16 (over z, core).
Axes of the slice: x: 4, y: 4, z: 8, core: 2. Of those that a mesh axis runs over, the one named last changes fastest.
Arguments:
- params: float32 [14, 262144], P(None, 'scene'), may hold values from -3 to 3
- pixel_basis: float32 [512, 13, 256], P('view'), may hold values from -6 to 6
- tile_blocks: int32 [512, 16, 2], P('view', 'scene'), may hold values from 0 to 127
- depth_rank: int32 [512, 32], P('view'), may hold values from 0 to 31, each once within a row
- target: float32 [512, 256], P('view'), may hold values from -0.3 to 0.3
Outputs:
- step: float32 [14, 262144], P(None, 'scene')
- residual: float32 [512, 256], P('view')
Inputs may be any that keep to these rules, and one draw needn't show every extreme that they name: `tile_blocks`: index of a block among the 128 blocks held by the owner named by the second dimension; a tile may list a block more than once. `depth_rank`: each row is a permutation of the 32 slots; a lower rank lies in front.
All inputs are finite; a program needn't handle non-finite values.
Results may differ from a plain program's by a relative error of at most 0.0003.
Values sent between devices are 32-bit elements; how exact they have to be, the bound alone decides.
A program may use at most 128 MiB of HBM per device.

v0:
```python
import jax
import jax.numpy as jnp
from jax import lax
from jax.sharding import PartitionSpec as P

BLOCK_SIZE = 128
ITERS = 3


alpha_max = 0.004
damping = 0.1
ridge_term = 0.0001
highest = lax.Precision.HIGHEST


def local(params, pixel_basis, tile_blocks, depth_rank, target):
    param_count = params.shape[0]
    tile_count = pixel_basis.shape[0]
    owned_slots = tile_blocks.shape[2]
    block_width = BLOCK_SIZE
    blocks = params.shape[1] // block_width
    param_blocks = params.reshape(param_count, blocks, block_width)
    pair_ids = tile_blocks.reshape(tile_count * owned_slots)
    onehot = (pair_ids[:, None] == jnp.arange(blocks, dtype=jnp.int32)[None, :]).astype(jnp.float32)
    position = lax.broadcasted_iota(jnp.int32, (block_width, block_width), 0)
    later_index = lax.broadcasted_iota(jnp.int32, (block_width, block_width), 1)
    strict = (position < later_index).astype(jnp.float32)
    pieces = jnp.take(param_blocks, pair_ids, axis=1).reshape(
        param_count, tile_count, owned_slots, block_width
    )
    logits = jnp.einsum("tcq,ctjg->tjqg", pixel_basis, pieces[: param_count - 1], precision=highest)
    opacity = alpha_max * jax.nn.sigmoid(logits)
    log_keep = jnp.log1p(-opacity)
    inner_log = jnp.einsum("tjqg,gh->tjqh", log_keep, strict, precision=highest)
    colour, opacity, log_keep, inner_log = (pieces[param_count - 1], opacity, log_keep, inner_log)
    block_log = jnp.sum(log_keep, axis=3)
    all_logs = lax.all_gather(block_log, "scene", axis=1, tiled=True)
    own_rank = lax.dynamic_slice_in_dim(
        depth_rank, lax.axis_index("scene") * owned_slots, owned_slots, 1
    )
    earlier = (depth_rank[:, None, :] < own_rank[:, :, None]).astype(jnp.float32)
    front_log = jnp.einsum("tjl,tlq->tjq", earlier, all_logs, precision=highest)
    weight_now = jnp.exp(front_log[:, :, :, None] + inner_log) * opacity
    slope_now = weight_now * colour[:, :, None, :] * (1.0 - opacity / alpha_max)
    weight = weight_now
    slopes = slope_now
    render_part = jnp.sum(weight * colour[:, :, None, :], axis=(1, 3))
    render = lax.psum(render_part, "scene")
    residual = render - target

    def to_blocks(feature, colour_term):
        stacked = jnp.concatenate([feature, colour_term[None]], axis=0)
        stacked = stacked.reshape(param_count, tile_count * owned_slots, block_width)
        return jnp.einsum("cpg,pb->cbg", stacked, onehot, precision=highest)

    def transpose_apply(weight_now, slope_now, pixel_vec):
        spread = pixel_vec[:, None, :, None]
        feature = jnp.einsum("tcq,tjqg->ctjg", pixel_basis, slope_now * spread, precision=highest)
        colour_term = jnp.sum(weight_now * spread, axis=2)
        return to_blocks(feature, colour_term)

    grad_part = transpose_apply(weight, slopes, residual)
    diag_feature = jnp.einsum(
        "tcq,tjqg->ctjg", pixel_basis * pixel_basis, slopes * slopes, precision=highest
    )
    diag_part = to_blocks(diag_feature, jnp.sum(weight * weight, axis=2))
    gradient, curv_diag = lax.psum((grad_part, diag_part), "view")

    def inner_sum(first_vec, second_vec):
        local_sum = jnp.sum(first_vec * second_vec)
        return lax.psum(local_sum, "scene")

    precondition = (1.0 + damping) * curv_diag + ridge_term
    solution = jnp.zeros_like(gradient)
    remainder = -gradient
    scaled = remainder / precondition
    direction = scaled
    rho_now = inner_sum(remainder, scaled)
    for iteration in range(ITERS):
        full_dir = direction
        forward_pieces = jnp.take(full_dir, pair_ids, axis=1).reshape(
            param_count, tile_count, owned_slots, block_width
        )
        projected = jnp.einsum(
            "tcq,ctjg->tjqg", pixel_basis, forward_pieces[: param_count - 1], precision=highest
        )
        partial_value = jnp.sum(
            slopes * projected + weight * forward_pieces[param_count - 1][:, :, None, :],
            axis=(1, 3),
        )
        curvature_pixel_vec = lax.psum(partial_value, "scene")
        curvature_partial_value = transpose_apply(weight, slopes, curvature_pixel_vec)
        reduced = lax.psum(curvature_partial_value, "view")
        image_dir = reduced + (damping * curv_diag + ridge_term) * direction
        step_size = rho_now / inner_sum(direction, image_dir)
        solution = solution + step_size * direction
        if iteration + 1 < ITERS:
            remainder = remainder - step_size * image_dir
            scaled = remainder / precondition
            rho_next = inner_sum(remainder, scaled)
            direction = scaled + rho_next / rho_now * direction
            rho_now = rho_next
    return (solution.reshape(param_count, blocks * block_width), residual)


def solution(mesh):
    in_specs = (
        P(None, "scene"),
        P("view", None, None),
        P("view", "scene", None),
        P("view", None),
        P("view", None),
    )
    out_specs = (P(None, "scene"), P("view", None))
    return jax.shard_map(local, mesh=mesh, in_specs=in_specs, out_specs=out_specs, check_vma=False)
```

profile of v0, /device:TPU:1, one launch (start us, length us, event | category | flops | bytes accessed | tf_op | source)
XLA Modules:
  0.0 938.0 jit_solution(4138145236380710642)
XLA Ops:
  7.2 0.8 copy.110
  8.1 1.4 copy.173
  9.6 0.5 copy.111
  10.2 0.6 gather_fusion
  11.0 14.0 %fusion.19 = (f32[32,2,256]{2,1,0:T(2,128)S(1)}, f32[32,2,128,256]{3,2,1,0:T(8,128)}) fusion(f32[13,32,2,128]{3,0,2,1:T(8,128)S(1)} %bitcast.140, f32[32,13,256,1]{2,0,1,3:T(8,128)} %bitcast.120), kind=kOutput, calls=%fused_computation.35 | convolution fusion | flops 339722240 | bytes 9306112 | tf_op jit(solution)/shard_map/tcq,ctjg->tjqg/dot_general | solution.py:31
  25.0 0.6 copy.113
  25.7 0.3 all-reduce.13.cloned.1.call-start
  26.1 42.5 %all-gather.2.cloned.1.call-done = f32[32,32,256]{2,0,1:T(8,128)} async-done(((f32[32,2,256]{2,0,1:T(8,128)}), f32[32,32,256]{2,0,1:T(8,128)}) %all-gather.2.cloned.1.call-update) | async-done | bytes 1048592 | tf_op jit(solution)/shard_map/all_gather | solution.py:37
  68.6 2.2 fusion.27
  70.8 18.9 %bitcast_multiply_fusion.3 = (f32[32,2,256,128]{2,3,1,0:T(8,128)}, f32[32,256]{1,0:T(8,128)S(1)}, f32[32,2,256,128]{2,3,1,0:T(8,128)}) fusion(f32[32,2,128,256]{3,2,1,0:T(8,128)} %get-tuple-element.14, f32[32,2,128]{2,1,0:T(2,128)S(1)} %bitcast.146, f32[32,2,256]{2,1,0:T(2,128)S(1)} %fusion.27), kind=kOutput, calls=%fused_computation.13 | convolution fusion | flops 3240108032 | bytes 25296896 | tf_op jit(solution)/shard_map/tjqg,gh->tjqh/dot_general | solution.py:34
  89.8 43.5 %psum.105 = f32[32,256]{1,0:T(8,128)S(1)} all-reduce(f32[32,256]{1,0:T(8,128)S(1)} %get-tuple-element.12), channel_id=1, replica_groups=mesh['view'=16,'scene'=16] {'scene'}, use_global_device_ids=true, to_apply=%region_2.4 | all-reduce | flops 8192 | bytes 65536 | tf_op jit(solution)/shard_map/psum | solution.py:48
  133.3 10.4 %fusion.15 = f32[32,2,128,13]{2,3,1,0:T(8,128)S(1)} fusion(f32[32,2,256,128]{2,3,1,0:T(8,128)} %get-tuple-element.11, f32[32,256]{1,0:T(8,128)S(1)} %sub.13, f32[32,13,256,1]{2,0,1,3:T(8,128)S(1)} %bitcast.121), kind=kOutput, calls=%fused_computation.30 | convolution fusion | flops 329252864 | bytes 9273344 | tf_op jit(solution)/shard_map/tcq,tjqg->ctjg/dot_general | solution.py:58
  143.7 0.1 copy.119
  143.9 2.3 multiply_reduce_fusion.4
  146.3 7.5 fusion.13
  153.8 0.1 copy.122
  154.0 1.6 convolution_bitcast_fusion.4
  155.5 1.5 convolution_bitcast_fusion.3
  157.1 101.0 %all-reduce.13.cloned.1.call-done = (f32[14,128,128]{2,1,0:T(8,128)}, f32[14,128,128]{2,1,0:T(8,128)}) async-done(((f32[14,128,128]{2,1,0:T(8,128)}, f32[14,128,128]{2,1,0:T(8,128)}), (f32[14,128,128]{2,1,0:T(8,128)}, f32[14,128,128]{2,1,0:T(8,128)})) %all-reduce.13.cloned.1.call-update) | async-done | bytes 1835024 | tf_op jit(solution)/shard_map/psum | solution.py:67
  258.2 1.6 negate_divide_fusion
  259.8 0.5 copy.123
  260.4 0.6 gather_fusion.1
  261.2 12.3 %fusion.5 = f32[32,256]{1,0:T(8,128)S(1)} fusion(f32[32,2,256,128]{2,3,1,0:T(8,128)} %get-tuple-element.11, f32[32,2,256,128]{2,3,1,0:T(8,128)} %get-tuple-element.15, f32[32,2,128]{2,1,0:T(2,128)S(1)} %bitcast.147, f32[13,32,2,128]{3,0,2,1:T(8,128)S(1)} %bitcast.131, f32[32,13,256,1]{2,0,1,3:T(8,128)S(1)} %bitcast.122), kind=kOutput, calls=%fused_computation.12 | convolution fusion | flops 335536128 | bytes 17694720 | tf_op jit(solution)/shard_map/tcq,ctjg->tjqg/dot_general | solution.py:84
  273.5 45.5 %psum.109 = f32[32,256]{1,0:T(8,128)S(1)} all-reduce(f32[32,256]{1,0:T(8,128)S(1)} %fusion.5), channel_id=1, replica_groups=mesh['view'=16,'scene'=16] {'scene'}, use_global_device_ids=true, to_apply=%region_10.12 | all-reduce | flops 8192 | bytes 65536 | tf_op jit(solution)/shard_map/psum | solution.py:91
  318.9 10.0 %fusion.11 = f32[32,2,128,13]{2,3,1,0:T(8,128)S(1)} fusion(f32[32,2,256,128]{2,3,1,0:T(8,128)} %get-tuple-element.11, f32[32,256]{1,0:T(8,128)S(1)} %psum.109, f32[32,13,256,1]{2,0,1,3:T(8,128)S(1)} %bitcast.123), kind=kOutput, calls=%fused_computation.24 | convolution fusion | flops 329252864 | bytes 9273344 | tf_op jit(solution)/shard_map/tcq,tjqg->ctjg/dot_general | solution.py:58
  328.9 4.6 multiply_reduce_fusion.2
  333.5 0.1 copy.127
  333.6 1.6 convolution_bitcast_fusion.2
  335.2 96.4 %all-reduce.7.cloned.1.call-done = f32[14,128,128]{2,1,0:T(8,128)} async-done(((f32[14,128,128]{2,1,0:T(8,128)}), f32[14,128,128]{2,1,0:T(8,128)}) %all-reduce.7.cloned.1.call-update) | async-done | bytes 917520 | tf_op jit(solution)/shard_map/psum | solution.py:93
  431.7 2.3 multiply_reduce_fusion.10
  433.9 26.2 %all-reduce = (f32[]{:T(128)}, f32[]{:T(128)}) all-reduce(f32[]{:T(128)} %get-tuple-element.6, f32[]{:T(128)} %get-tuple-element.5), channel_id=1, replica_groups=mesh['view'=16,'scene'=16] {'scene'}, use_global_device_ids=true, to_apply=%region_8.10 | all-reduce | flops 2 | bytes 16 | tf_op jit(solution)/shard_map/psum | solution.py:71
  461.5 2.2 multiply_reduce_fusion.9
  463.7 25.1 %psum.112 = f32[]{:T(128)} all-reduce(f32[]{:T(128)} %multiply_reduce_fusion.9), channel_id=1, replica_groups=mesh['view'=16,'scene'=16] {'scene'}, use_global_device_ids=true, to_apply=%region_16.18 | all-reduce | flops 1 | bytes 8 | tf_op jit(solution)/shard_map/psum | solution.py:71
  490.1 1.6 multiply_add_fusion.3
  491.8 1.5 copy.128
  493.3 2.6 gather_fusion.2
  495.9 1.2 select_bitcast_fusion.1
  497.1 12.1 %fusion.3 = f32[32,256]{1,0:T(8,128)S(1)} fusion(f32[32,2,256,128]{2,3,1,0:T(8,128)} %get-tuple-element.11, f32[32,2,256,128]{2,3,1,0:T(8,128)} %get-tuple-element.15, f32[32,2,128]{2,1,0:T(2,128)S(1)} %bitcast.148, f32[13,32,2,128]{3,0,2,1:T(8,128)S(1)} %bitcast.132, f32[32,13,256,1]{2,0,1,3:T(8,128)S(1)} %bitcast.124), kind=kOutput, calls=%fused_computation.9 | convolution fusion | flops 335536128 | bytes 17694720 | tf_op jit(solution)/shard_map/tcq,ctjg->tjqg/dot_general | solution.py:84
  509.2 42.8 %psum.113 = f32[32,256]{1,0:T(8,128)S(1)} all-reduce(f32[32,256]{1,0:T(8,128)S(1)} %fusion.3), channel_id=1, replica_groups=mesh['view'=16,'scene'=16] {'scene'}, use_global_device_ids=true, to_apply=%region_18.20 | all-reduce | flops 8192 | bytes 65536 | tf_op jit(solution)/shard_map/psum | solution.py:91
  552.0 9.8 %fusion.9 = f32[32,2,128,13]{2,3,1,0:T(8,128)S(1)} fusion(f32[32,2,256,128]{2,3,1,0:T(8,128)} %get-tuple-element.11, f32[32,256]{1,0:T(8,128)S(1)} %psum.113, f32[32,13,256,1]{2,0,1,3:T(8,128)S(1)} %bitcast.125), kind=kOutput, calls=%fused_computation.21 | convolution fusion | flops 329252864 | bytes 9273344 | tf_op jit(solution)/shard_map/tcq,tjqg->ctjg/dot_general | solution.py:58
  561.8 4.6 multiply_reduce_fusion.1
  566.4 0.1 copy.132
  566.6 1.6 convolution_bitcast_fusion.1
  568.2 95.9 %all-reduce.9.cloned.1.call-done = f32[14,128,128]{2,1,0:T(8,128)} async-done(((f32[14,128,128]{2,1,0:T(8,128)}), f32[14,128,128]{2,1,0:T(8,128)}) %all-reduce.9.cloned.1.call-update) | async-done | bytes 917520 | tf_op jit(solution)/shard_map/psum | solution.py:93
  664.1 2.0 multiply_reduce_fusion.8
  666.2 26.2 %psum.115 = f32[]{:T(128)} all-reduce(f32[]{:T(128)} %multiply_reduce_fusion.8), channel_id=1, replica_groups=mesh['view'=16,'scene'=16] {'scene'}, use_global_device_ids=true, to_apply=%region_22.24 | all-reduce | flops 1 | bytes 8 | tf_op jit(solution)/shard_map/psum | solution.py:71
  693.6 2.6 multiply_reduce_fusion.7
  696.2 25.2 %psum.116 = f32[]{:T(128)} all-reduce(f32[]{:T(128)} %multiply_reduce_fusion.7), channel_id=1, replica_groups=mesh['view'=16,'scene'=16] {'scene'}, use_global_device_ids=true, to_apply=%region_24.26 | all-reduce | flops 1 | bytes 8 | tf_op jit(solution)/shard_map/psum | solution.py:71
  722.7 2.0 multiply_add_fusion.1
  724.8 0.9 copy-done.4
  725.7 1.5 copy.133
  727.2 2.6 gather_fusion.3
  729.8 1.2 select_bitcast_fusion
  731.0 12.1 %fusion.1 = f32[32,256]{1,0:T(8,128)S(1)} fusion(f32[32,2,256,128]{2,3,1,0:T(8,128)} %get-tuple-element.11, f32[32,2,256,128]{2,3,1,0:T(8,128)} %get-tuple-element.15, f32[32,2,128]{2,1,0:T(2,128)S(1)} %bitcast.149, f32[13,32,2,128]{3,0,2,1:T(8,128)S(1)} %bitcast.130, f32[32,13,256,1]{2,0,1,3:T(8,128)S(1)} %bitcast.126), kind=kOutput, calls=%fused_computation.6 | convolution fusion | flops 335536128 | bytes 17694720 | tf_op jit(solution)/shard_map/tcq,ctjg->tjqg/dot_general | solution.py:84
  743.1 42.8 %psum.117 = f32[32,256]{1,0:T(8,128)S(1)} all-reduce(f32[32,256]{1,0:T(8,128)S(1)} %fusion.1), channel_id=1, replica_groups=mesh['view'=16,'scene'=16] {'scene'}, use_global_device_ids=true, to_apply=%region_26.28 | all-reduce | flops 8192 | bytes 65536 | tf_op jit(solution)/shard_map/psum | solution.py:91
  785.9 9.8 %fusion.7 = f32[32,2,128,13]{2,3,1,0:T(8,128)S(1)} fusion(f32[32,2,256,128]{2,3,1,0:T(8,128)} %get-tuple-element.11, f32[32,256]{1,0:T(8,128)S(1)} %psum.117, f32[32,13,256,1]{2,0,1,3:T(8,128)S(1)} %bitcast.127), kind=kOutput, calls=%fused_computation.18 | convolution fusion | flops 329252864 | bytes 9273344 | tf_op jit(solution)/shard_map/tcq,tjqg->ctjg/dot_general | solution.py:58
  795.8 4.6 multiply_reduce_fusion
  800.3 0.1 copy.137
  800.5 1.6 convolution_bitcast_fusion
  802.1 96.0 %all-reduce.11.cloned.1.call-done = f32[14,128,128]{2,1,0:T(8,128)} async-done(((f32[14,128,128]{2,1,0:T(8,128)}), f32[14,128,128]{2,1,0:T(8,128)}) %all-reduce.11.cloned.1.call-update) | async-done | bytes 917520 | tf_op jit(solution)/shard_map/psum | solution.py:93
  898.1 2.3 multiply_reduce_fusion.6
  900.4 26.2 %psum.119 = f32[]{:T(128)} all-reduce(f32[]{:T(128)} %multiply_reduce_fusion.6), channel_id=1, replica_groups=mesh['view'=16,'scene'=16] {'scene'}, use_global_device_ids=true, to_apply=%region_30.32 | all-reduce | flops 1 | bytes 8 | tf_op jit(solution)/shard_map/psum | solution.py:71
  927.9 1.5 multiply_add_fusion
  929.5 1.6 copy.174
  (44 shorter events, 1.1 us)
Async XLA Ops:
  7.2 61.4 %all-gather.2.cloned.1.call-start = ((), (), s32[]{:S(2)}) async-start(), calls=%async_computation | async-start | bytes 1114112 | tf_op jit(solution)/shard_map/all_gather | solution.py:37
  11.0 15.0 %copy-start.6 = (s32[32,32]{1,0:T(8,128)S(1)}, s32[32,32]{1,0:T(8,128)}, u32[]{:S(2)}) copy-start(s32[32,32]{1,0:T(8,128)} %param.10) | copy-start | bytes 12292
  11.0 15.1 %copy-start.3 = (f32[32,13,256]{2,0,1:T(8,128)S(1)}, f32[32,13,256]{2,0,1:T(8,128)}, u32[]{:S(2)}) copy-start(f32[32,13,256]{2,0,1:T(8,128)} %param.8) | copy-start | bytes 1277956
  25.7 232.5 %all-reduce.13.cloned.1.call-start = ((), (), s32[]{:S(2)}) async-start(), calls=%async_computation.4 | async-start | bytes 3670016 | tf_op jit(solution)/shard_map/psum | solution.py:67
  70.8 62.5 %copy-start.7 = (f32[32,256]{1,0:T(8,128)S(1)}, f32[32,256]{1,0:T(8,128)}, u32[]{:S(2)}) copy-start(f32[32,256]{1,0:T(8,128)} %param.11) | copy-start | bytes 98308
  133.3 10.6 %copy-start = (f32[32,2,256,128]{2,3,1,0:T(8,128)S(1)}, f32[32,2,256,128]{2,3,1,0:T(8,128)}, u32[]{:S(2)}) copy-start(f32[32,2,256,128]{2,3,1,0:T(8,128)} %get-tuple-element.15) | copy-start | bytes 25165828
  133.3 12.9 %copy-start.5 = (f32[32,256]{1,0:T(8,128)}, f32[32,256]{1,0:T(8,128)S(1)}, u32[]{:S(2)}) copy-start(f32[32,256]{1,0:T(8,128)S(1)} %sub.13) | copy-start | bytes 98308
  133.3 12.9 %slice-start = ((s8[8388608]{0:T(1024)(128)(4,1)}), s8[4194304]{0:T(1024)(128)(4,1)S(1)}, s32[]{:S(2)}) async-start(s8[8388608]{0:T(1024)(128)(4,1)} %bitcast.118), calls=%async_computation.5 | async-start | bytes 8388608
  133.3 12.9 %slice-start.1 = ((s8[8388608]{0:T(1024)(128)(4,1)}), s8[4194304]{0:T(1024)(128)(4,1)S(1)}, s32[]{:S(2)}) async-start(s8[8388608]{0:T(1024)(128)(4,1)} %bitcast.118), calls=%async_computation.6 | async-start | bytes 8388608
  157.1 274.6 %all-reduce.7.cloned.1.call-start = ((), (), s32[]{:S(2)}) async-start(), calls=%async_computation.1 | async-start | bytes 1835008 | tf_op jit(solution)/shard_map/psum | solution.py:93
  318.9 112.7 %copy-start.1 = (f32[14,128,128]{2,1,0:T(8,128)S(1)}, f32[14,128,128]{2,1,0:T(8,128)}, u32[]{:S(2)}) copy-start(f32[14,128,128]{2,1,0:T(8,128)} %get-tuple-element.9) | copy-start | bytes 2752516
  318.9 112.7 %copy-start.2 = (f32[14,128,128]{2,1,0:T(8,128)S(1)}, f32[14,128,128]{2,1,0:T(8,128)}, u32[]{:S(2)}) copy-start(f32[14,128,128]{2,1,0:T(8,128)} %get-tuple-element.10) | copy-start | bytes 2752516
  335.2 328.9 %all-reduce.9.cloned.1.call-start = ((), (), s32[]{:S(2)}) async-start(), calls=%async_computation.2 | async-start | bytes 1835008 | tf_op jit(solution)/shard_map/psum | solution.py:93
  568.1 329.9 %all-reduce.11.cloned.1.call-start = ((), (), s32[]{:S(2)}) async-start(), calls=%async_computation.3 | async-start | bytes 1835008 | tf_op jit(solution)/shard_map/psum | solution.py:93
  724.7 0.9 copy-start.4
Sparse Core Ops, SparseCore 0:
  25.8 42.7 all-gather.1
  157.2 100.9 all-reduce.12
  335.3 96.2 all-reduce.6
  568.3 95.8 all-reduce.8
  802.2 95.8 all-reduce.10
where the time goes:
time: 944 us; the launch traced here: 938 us
  waiting for transfers between devices  432 us (46%)
  blocking collectives  304 us (32%)
  matrix products  127 us (13%)
  other arithmetic  36.9 us (4%)
  between operations  21.2 us (2%)
  local copies, waits for them, and re-layouts  17.1 us (2%)
    psum x3, waiting for transfers between devices, local(): reduced = lax.psum(curvature_partial_value, 'view')  288 us
    psum x3, blocking collectives, local(): curvature_pixel_vec = lax.psum(partial_value, 'scene')  131 us
    psum x5, blocking collectives, inner_sum(): return lax.psum(local_sum, 'scene')  129 us
    psum x1, waiting for transfers between devices, local(): gradient, curv_diag = lax.psum((grad_part, diag_part), 'view')  101 us
    psum x1, blocking collectives, local(): render = lax.psum(render_part, 'scene')  43.5 us
    all_gather x1, waiting for transfers between devices, local(): all_logs = lax.all_gather(block_log, 'scene', axis=1, tiled=True)  42.5 us
    dot_general x4, matrix products, transpose_apply(): jnp.einsum('tcq,tjqg->ctjg', pixel_basis, slope_now * spread, precision=h...  40 us
    dot_general x3, matrix products, local(): jnp.einsum('tcq,ctjg->tjqg', pixel_basis, forward_pieces[:param_count - 1...  36.4 us
  transfers between devices with their start and end apart: 5, of which 5 were waited for; matrix products, arithmetic and copies ran while one was open for 0% of the time, Pallas kernels for 0%

commit v1 on v0

v1 whole, which is shorter than its diff:
```python
import functools

import jax
import jax.numpy as jnp
from jax import lax
from jax.experimental import pallas as pl
from jax.experimental.pallas import tpu as pltpu
from jax.sharding import PartitionSpec as P

MESH = pl.DeviceIdType.MESH
ALPHA = 0.004
DAMPING = 0.1
RIDGE = 0.0001
ITERS = 3
G = 128
CP = 16
f32 = jnp.float32
bf16 = jnp.bfloat16
NT = (((1,), (1,)), ((), ()))
TN = (((0,), (0,)), ((), ()))


def split2(x):
    hi = x.astype(bf16)
    return hi, (x - hi.astype(f32)).astype(bf16)


def split3(x):
    hi = x.astype(bf16)
    rest = x - hi.astype(f32)
    mid = rest.astype(bf16)
    return hi, mid, (rest - mid.astype(f32)).astype(bf16)


def dot(a, b, dims=(((1,), (0,)), ((), ()))):
    return lax.dot_general(a, b, dims, preferred_element_type=f32)


def lanes(ref, row):
    return jnp.concatenate([ref[pl.ds(row, 1), :], ref[pl.ds(row + 1, 1), :]], axis=1)


def kernel(
    n, params, tiles,
    par, basis, ids, ids_rows, rank, target,
    step, residual,
    b16, bst, S, W, hi, lo, stk, onehot,
    bl_out, bl_in, fr_out, fr_in,
    u_out, u_in, s_out, u_all, u_now,
    w_out, rs_in, z, direction, total_step, z_flat, z_shard, shard,
    dot_out, dot_in,
    send_sem, recv_sem,
):
    view = lax.axis_index("view")
    scene = lax.axis_index("scene")
    barrier = pltpu.get_barrier_semaphore()

    def greet(d, c):
        pl.semaphore_signal(barrier, inc=1, device_id=(lax.rem(view + d, n), scene), device_id_type=MESH)
        pl.semaphore_signal(barrier, inc=1, device_id=(view, lax.rem(scene + d, n)), device_id_type=MESH)
        return c

    lax.fori_loop(1, n, greet, 0)


    def send(axis, phase, src_of, dst):
        def body(d, c):
            if axis == "view":
                peer = lax.rem(view + d, n)
                where = (peer, scene)
            else:
                peer = lax.rem(scene + d, n)
                where = (view, peer)
            pltpu.make_async_remote_copy(
                src_ref=src_of(peer), dst_ref=dst, send_sem=send_sem.at[phase], recv_sem=recv_sem.at[phase],
                device_id=where, device_id_type=MESH,
            ).start()
            return c

        lax.fori_loop(1, n, body, 0)

    def wait(phase, received, sent=None):
        sent = received if sent is None else sent
        pltpu.make_async_copy(received, received, recv_sem.at[phase]).wait()
        pltpu.make_async_copy(sent, sent, send_sem.at[phase]).wait()

    block_at = lax.broadcasted_iota(jnp.int32, (G, tiles), 0)
    hot = [jnp.where(block_at == ids_rows[pl.ds(j, 1), :], 1.0, 0.0).astype(bf16) for j in range(2)]
    onehot[...] = jnp.concatenate(hot + hot, axis=1)
    below = lax.broadcasted_iota(jnp.int32, (G, G), 1) < lax.broadcasted_iota(jnp.int32, (G, G), 0)
    below = jnp.where(below, 1.0, 0.0).astype(bf16)
    below = jnp.concatenate([below, below], axis=1)

    halves = [w_out.at[h].reshape(CP * G, G) for h in range(2)]
    for h in range(2):
        halves[h][pl.ds(0, (params - 1) * tiles)] = basis[:, G * h : G * (h + 1)]

    def prepare(t, c):
        full = jnp.concatenate([half[pl.ds(t, params - 1, stride=tiles), :] for half in halves], axis=1)
        full = jnp.concatenate([full, jnp.zeros((CP - params + 1, full.shape[1]), f32)], axis=0)
        b16[t] = full
        bh, bl = split2(full)
        bst[t] = jnp.concatenate([bh, bh, bl], axis=0)
        return c

    lax.fori_loop(0, tiles, prepare, 0)

    def stage(b, c):
        piece = par[:, pl.ds(pl.multiple_of(b * G, G), G)]
        direction[b] = jnp.concatenate([piece, jnp.zeros((CP - params, G), f32)], axis=0)
        return c

    lax.fori_loop(0, G, stage, 0, unroll=4)
    z_flat[8 * (params + 1) :] = jnp.zeros((8 * (CP - params - 1), G), f32)

    def listing_params(t, j):
        return direction[ids[j, t]]

    def slot_row(t, j):
        return 8 * (t // 2) + 4 * j + 2 * lax.rem(t, 2)

    def opacities(t, c):
        bh, bm, bl = split3(b16[t])
        rhs = jnp.concatenate([bh, bm, bh, bl, bh, bm], axis=0)
        for j in range(2):
            p = 2 * t + j
            vh, vm, vl = split3(listing_params(t, j))
            lhs = jnp.concatenate([vh, vh, vm, vh, vl, vm], axis=0)
            logit = dot(lhs, rhs, TN)
            o = ALPHA * (1.0 / (1.0 + jnp.exp(-logit)))
            keep = -o * (1.0 + o * (0.5 + o * (1.0 / 3.0 + o * 0.25)))
            W[p] = o
            kh, kl = split2(keep)
            hi[p, :, :256] = kh
            lo[p, :, :256] = kl
            total = jnp.sum(keep, axis=0, keepdims=True)
            r = slot_row(t, j)
            bl_out[pl.ds(r, 1), :] = total[:, :G]
            bl_out[pl.ds(r + 1, 1), :] = total[:, G:]
        return c

    lax.fori_loop(0, tiles, opacities, 0, unroll=2)

    pl.semaphore_wait(barrier, 2 * (n - 1))
    rows8 = lambda ref, i: ref.at[pl.ds(pl.multiple_of(i * 8, 8), 8)]
    some8 = lambda ref: ref.at[pl.ds(0, 8 * (n - 1))]
    send("scene", 0, lambda peer: rows8(bl_out, peer), rows8(bl_in, scene))
    rows8(bl_in, scene)[...] = rows8(bl_out, scene)[...]

    def weights(t, c):
        for j in range(2):
            p = 2 * t + j
            keeps = jnp.concatenate([hi[p, :, :256], lo[p, :, :256]], axis=0)
            inner = dot(below, keeps)
            o = W[p]
            colour = jnp.transpose(listing_params(t, j))[:, params - 1 : params]
            w = jnp.exp(inner) * o
            W[p] = w
            S[p] = w * colour * (1.0 - o * (1.0 / ALPHA))
        return c

    lax.fori_loop(0, tiles // 2, weights, 0)

    wait(0, some8(bl_in), some8(bl_out))
    slots = 2 * n
    eye = lax.broadcasted_iota(jnp.int32, (slots, slots), 0) == lax.broadcasted_iota(jnp.int32, (slots, slots), 1)
    for i in range(2):
        rank_row = jnp.broadcast_to(rank[pl.ds(2 * scene + i, 1), :].astype(f32), (slots, slots))
        rank_col = jnp.sum(jnp.where(eye, rank_row, 0.0), axis=1, keepdims=True)
        earlier = jnp.where(rank_row < rank_col, 1.0, 0.0).astype(bf16)
        for h in range(2):
            lh, lm, ll = split3(bl_in[pl.ds(2 * i + h, slots, stride=4), :])
            front = dot(earlier, lh) + dot(earlier, lm) + dot(earlier, ll)
            fr_out[pl.ds(2 * i + h, slots, stride=4), :] = jnp.exp(front)
    send("scene", 1, lambda peer: rows8(fr_out, peer), rows8(fr_in, scene))
    rows8(fr_in, scene)[...] = rows8(fr_out, scene)[...]

    lax.fori_loop(tiles // 2, tiles, weights, 0)
    wait(1, some8(fr_in), some8(fr_out))

    def u_row(t):
        return 8 * (t // 2) + 2 * lax.rem(t, 2)

    def put_u(t, value):
        r = u_row(t)
        u_out[pl.ds(r, 1), :] = value[:, :G]
        u_out[pl.ds(r + 1, 1), :] = value[:, G:]

    def finish(t, c):
        total = jnp.zeros((1, 2 * G), f32)
        for j in range(2):
            p = 2 * t + j
            factor = lanes(fr_in, slot_row(t, j))
            w = W[p] * factor
            s = S[p] * factor
            W[p] = w
            S[p] = s
            sh, sl = split2(s)
            wh, wl = split2(w)
            hi[p, :, :256] = sh
            hi[p, :, 256:] = wh
            lo[p, :, :256] = sl
            lo[p, :, 256:] = wl
            colour = jnp.transpose(listing_params(t, j))[:, params - 1 : params]
            total = total + jnp.sum(w * colour, axis=0, keepdims=True)
        put_u(t, total)
        return c

    u_out[...] = jnp.zeros_like(u_out)
    lax.fori_loop(0, tiles, finish, 0, unroll=2)

    def scene_scatter(phase, k):
        rows = u_in.at[k]
        send("scene", phase, lambda peer: rows8(u_out, peer), rows8(rows, scene))
        rows8(rows, scene)[...] = rows8(u_out, scene)[...]

    def scene_gather(phase, k):
        wait(phase, some8(u_in.at[k]), some8(u_out))
        total = u_in[k, pl.ds(0, 8), :]
        for i in range(1, n):
            total = total + u_in[k, pl.ds(8 * i, 8), :]
        s_out[...] = total
        send("scene", phase + 1, lambda peer: s_out, rows8(u_all.at[k], scene))
        rows8(u_all.at[k], scene)[...] = total

    def scene_done(phase, k):
        wait(phase + 1, some8(u_all.at[k]))

    def scatter_blocks(slot):
        for c in range(0, params, 2):
            x = jnp.concatenate([stk[pl.ds((c + e) * 2 * tiles, 2 * tiles), :] for e in range(2)], axis=1)
            xh, xl = split2(x)
            out = dot(onehot[...], jnp.concatenate([xh, xl], axis=0))
            w_out[slot, c] = out[:, :G]
            w_out[slot, c + 1] = out[:, G:]

    def put_listing(t, value):
        for j in range(2):
            stk[pl.ds(tiles * j + t, CP, stride=2 * tiles), :] = value[:, G * j : G * (j + 1)]

    blocks8 = lambda ref, i: ref.at[:, pl.ds(pl.multiple_of(i * 8, 8), 8), :]
    most_blocks = lambda ref: ref.at[:, pl.ds(0, 8 * (n - 1)), :]

    def view_scatter(phase, slot, k):
        out = w_out.at[slot, pl.ds(0, params + 1)]
        send("view", phase, lambda peer: blocks8(out, peer), rs_in.at[k, view])
        rs_in[k, view] = w_out[slot, pl.ds(0, params + 1), pl.ds(pl.multiple_of(view * 8, 8), 8), :]

    def view_total(phase, slot, k):
        wait(phase, rs_in.at[k, pl.ds(0, n - 1)], most_blocks(w_out.at[slot, pl.ds(0, params + 1)]))
        return lax.fori_loop(1, n, lambda i, a: a + rs_in[k, i], rs_in[k, 0])

    is_colour = lax.broadcasted_iota(jnp.int32, (CP, 256), 0) == params - 1

    def transpose_rows(left_s, left_w, right_hi, right_lo):
        sh, sl = split2(left_s)
        wh, wl = split2(left_w)
        high = jnp.concatenate([sh, wh], axis=1)
        both = jnp.concatenate([high, jnp.concatenate([sl, wl], axis=1)], axis=0)
        first = dot(both, right_hi, NT)
        return first[:CP] + first[CP:] + dot(high, right_lo, NT)

    scene_scatter(2, 0)

    def diagonal(t, c):
        left_s = b16[t] * b16[t]
        left_w = jnp.where(is_colour, 1.0, 0.0)
        parts = []
        for j in range(2):
            p = 2 * t + j
            sh, sl = split2(S[p] * S[p])
            wh, wl = split2(W[p] * W[p])
            parts.append(transpose_rows(
                left_s, left_w, jnp.concatenate([sh, wh], axis=1), jnp.concatenate([sl, wl], axis=1)))
        put_listing(t, jnp.concatenate(parts, axis=1))
        return c

    lax.fori_loop(0, tiles // 2, diagonal, 0, unroll=2)
    scene_gather(2, 0)
    lax.fori_loop(tiles // 2, tiles, diagonal, 0, unroll=2)
    scatter_blocks(0)
    w_out[0, params] = jnp.zeros((G, G), f32)
    view_scatter(4, 0, 0)
    scene_done(2, 0)

    def apply_transpose(t, u):
        left_s = b16[t] * u
        left_w = jnp.where(is_colour, u, 0.0)
        right_hi = jnp.concatenate([hi[2 * t], hi[2 * t + 1]], axis=0)
        right_lo = jnp.concatenate([lo[2 * t], lo[2 * t + 1]], axis=0)
        put_listing(t, transpose_rows(left_s, left_w, right_hi, right_lo))

    def gradient(t, c):
        u = lanes(u_all.at[0], u_row(t)) - target[pl.ds(t, 1), :]
        residual[pl.ds(t, 1), :] = u
        apply_transpose(t, u)
        return c

    lax.fori_loop(0, tiles, gradient, 0, unroll=4)
    scatter_blocks(1)
    w_out[1, params] = jnp.zeros((G, G), f32)
    view_scatter(5, 1, 1)

    pixel_row = lax.rem(lax.broadcasted_iota(jnp.int32, (8 * n, G), 0), 8) < 4
    R, Z, DP, D = 0, 1, 2, 3

    def lane_sum(x):
        return jnp.sum(x, axis=1, keepdims=True)

    diag = view_total(4, 0, 0)[:params]
    shard[D] = diag
    shard[R] = -view_total(5, 1, 1)[:params]

    def gather_z(k, phase):
        d = shard[D]
        r = shard[R]
        zs = r / ((1.0 + DAMPING) * d + RIDGE)
        dz = (DAMPING * d + RIDGE) * zs
        part = lambda x: jnp.sum(jnp.sum(x, axis=0), axis=0, keepdims=True)
        rows = [part(r * zs), part(zs * dz)]
        rows.append(part(shard[Z] * dz) if k else jnp.zeros((1, G), f32))
        rows.append(jnp.zeros((5, G), f32))
        z_flat[pl.ds(0, 8 * params)] = zs.reshape(8 * params, G)
        z_flat[pl.ds(8 * params, 8)] = jnp.concatenate(rows, axis=0)
        for i in range(8):
            z_shard[k, i] = z_flat[pl.ds(i, CP, stride=8), :]
        send("view", phase, lambda peer: z_shard.at[k], rows8(z.at[k], view))
        rows8(z.at[k], view)[...] = z_shard[k]
        return zs

    one = jnp.ones((1, 1), f32)
    rz_old, pdp = one, 0.0 * one
    phase = 6
    for k in range(ITERS):
        zs = gather_z(k, phase)
        wait(phase, some8(z.at[k]))
        phase += 1
        flat = z.at[k].reshape(CP * G, G)

        def forward(t, c):
            v = jnp.concatenate(
                [z[k, ids[j, t]] for j in range(2)], axis=1)
            vh, vl = split2(v)
            lhs = jnp.concatenate([vh, vl, vh], axis=0)
            total = jnp.zeros((1, 2 * G), f32)
            for j in range(2):
                p = 2 * t + j
                projected = dot(lhs[:, G * j : G * (j + 1)], bst[t], TN)
                tint = jnp.transpose(v[:, G * j : G * (j + 1)])[:, params - 1 : params]
                total = total + jnp.sum(S[p] * projected + W[p] * tint, axis=0, keepdims=True)
            put_u(t, total)
            return c

        lax.fori_loop(0, tiles, forward, 0, unroll=4)
        sums = [
            jnp.sum(flat[pl.ds(CP * i + params, n, stride=8 * CP), :], axis=0, keepdims=True) for i in range(3)]
        sums = jnp.concatenate(sums + [sums[0]], axis=0)
        for i in range(n):
            u_out[pl.ds(8 * i + 4, 4), :] = sums
        scene_scatter(phase, k + 1)
        scene_gather(phase, k + 1)
        scene_done(phase, k + 1)
        phase += 2
        totals = lane_sum(u_all[k + 1, pl.ds(4, 4), :])
        rz, zdz, zdp = totals[0:1], totals[1:2], totals[2:3]
        beta = rz / rz_old if k else 0.0 * one
        u = u_all[k + 1] + beta * u_now[...] if k else u_all[k + 1]
        u = jnp.where(pixel_row, u, 0.0)
        u_now[...] = u
        pdp = zdz + 2.0 * beta * zdp + beta * beta * pdp
        square = jnp.sum(u * u, axis=0, keepdims=True)
        if k:
            direction[...] = z[k] + beta * direction[...]
            shard[Z] = zs + beta * shard[Z]
        else:
            direction[...] = z[k]
            shard[Z] = zs
        if k + 1 < ITERS:
            lax.fori_loop(0, tiles, lambda t, c: (apply_transpose(t, lanes(u_now, u_row(t))), c)[1], 0, unroll=4)
            scatter_blocks(k)
            w_out[k, params] = jnp.broadcast_to(square, (G, G))
            view_scatter(phase, k, k + 2)
            w = view_total(phase, k, k + 2)
            phase += 1
            a = rz / (lane_sum(w[params, 0:1]) + pdp)
            image = w[:params] + (DAMPING * shard[D] + RIDGE) * shard[Z]
            shard[R] = shard[R] - a * image
        else:
            dot_out[...] = jnp.broadcast_to(square, (8, G))
            send("view", phase, lambda peer: dot_out, rows8(dot_in, view))
            rows8(dot_in, view)[...] = dot_out[...]
            wait(phase, some8(dot_in))
            total = dot_in[pl.ds(0, 1), :]
            for i in range(1, n):
                total = total + dot_in[pl.ds(8 * i, 1), :]
            a = rz / (lane_sum(total) + pdp)
        if k + 1 == ITERS:
            for b in range(G):
                step[:, pl.ds(b * G, G)] = (total_step[b] + a * direction[b])[:params]
        elif k:
            total_step[...] = total_step[...] + a * direction[...]
        else:
            total_step[...] = a * direction[...]
        rz_old = rz


def local(n, params, pixel_basis, tile_blocks, depth_rank, target):
    count = params.shape[0]
    tiles, _, pixels = pixel_basis.shape
    ids = tile_blocks.transpose(1, 2, 0).reshape(2, tiles)
    basis = pixel_basis.transpose(1, 0, 2).reshape((count - 1) * tiles, pixels)
    vmem = pl.BlockSpec(memory_space=pltpu.VMEM)
    lists = 2 * tiles
    phases = 6 + 4 * (ITERS - 1) + 4
    return pl.pallas_call(
        functools.partial(kernel, n, count, tiles),
        out_shape=(
            jax.ShapeDtypeStruct((count, G * G), f32),
            jax.ShapeDtypeStruct((tiles, pixels), f32),
        ),
        in_specs=[vmem, vmem, pl.BlockSpec(memory_space=pltpu.SMEM), vmem, vmem, vmem],
        out_specs=(vmem, vmem),
        scratch_shapes=[
            pltpu.VMEM((tiles, CP, pixels), f32),
            pltpu.VMEM((tiles, 3 * CP, pixels), bf16),
            pltpu.VMEM((lists, G, pixels), f32),
            pltpu.VMEM((lists, G, pixels), f32),
            pltpu.VMEM((lists, G, 2 * pixels), bf16),
            pltpu.VMEM((lists, G, 2 * pixels), bf16),
            pltpu.VMEM((CP * lists, G), f32),
            pltpu.VMEM((G, 2 * lists), bf16),
            pltpu.VMEM((8 * n, G), f32),
            pltpu.VMEM((8 * n, G), f32),
            pltpu.VMEM((8 * n, G), f32),
            pltpu.VMEM((8 * n, G), f32),
            pltpu.VMEM((8 * n, G), f32),
            pltpu.VMEM((ITERS + 1, 8 * n, G), f32),
            pltpu.VMEM((8, G), f32),
            pltpu.VMEM((ITERS + 1, 8 * n, G), f32),
            pltpu.VMEM((8 * n, G), f32),
            pltpu.VMEM((2, CP, G, G), f32),
            pltpu.VMEM((ITERS + 1, n, count + 1, 8, G), f32),
            pltpu.VMEM((ITERS, G, CP, G), f32),
            pltpu.VMEM((G, CP, G), f32),
            pltpu.VMEM((G, CP, G), f32),
            pltpu.VMEM((8 * CP, G), f32),
            pltpu.VMEM((ITERS, 8, CP, G), f32),
            pltpu.VMEM((4, count, 8, G), f32),
            pltpu.VMEM((8, G), f32),
            pltpu.VMEM((8 * n, G), f32),
            pltpu.SemaphoreType.DMA((phases,)),
            pltpu.SemaphoreType.DMA((phases,)),
        ],
        compiler_params=pltpu.CompilerParams(
            collective_id=0, has_side_effects=True, vmem_limit_bytes=64 * 1024 * 1024 - 65536),
        name="lm_step",
    )(params, basis, ids, ids, depth_rank, target)


def solution(mesh):
    in_specs = (
        P(None, "scene"),
        P("view", None, None),
        P("view", "scene", None),
        P("view", None),
        P("view", None),
    )
    out_specs = (P(None, "scene"), P("view", None))
    step = functools.partial(local, mesh.shape["scene"])
    return jax.shard_map(step, mesh=mesh, in_specs=in_specs, out_specs=out_specs, check_vma=False)
```

time: 944 us -> 211 us (0.22)
  waiting for transfers between devices: 432 us -> 0 us
  blocking collectives: 304 us -> 0 us
  Pallas kernels: 0 us -> 207 us
  matrix products: 127 us -> 0 us
  other arithmetic: 36.9 us -> 0 us
  between operations: 21.2 us -> 0.65 us
  local copies, waits for them, and re-layouts: 17.1 us -> 2.89 us
    psum x4 -> x0, waiting for transfers between devices: 389 us -> none  [the longest x3 288 us: local(): reduced = lax.psum(curvature_partial_value, 'view')]
    psum x9 -> x0, blocking collectives: 304 us -> none  [the longest x3 131 us: local(): curvature_pixel_vec = lax.psum(partial_value, 'scene')]
    pallas_call x0 -> x1, Pallas kernels: none -> 207 us  [local(): pl.pallas_call(functools.partial(kernel, n, count, tiles), out_shape=(jax...]
    dot_general x16 -> x0, matrix products: 127 us -> none  [the longest x4 40 us: transpose_apply(): jnp.einsum('tcq,tjqg->ctjg', pixel_basis, slope_now * spread, precision=h...]
    all_gather x1 -> x0, waiting for transfers between devices: 42.5 us -> none  [local(): all_logs = lax.all_gather(block_log, 'scene', axis=1, tiled=True)]
    reduce_sum x9 -> x0, other arithmetic: 27.4 us -> none  [the longest x4 16.1 us: transpose_apply(): colour_term = jnp.sum(weight_now * spread, axis=2)]
  transfers between devices with their start and end apart: 5 -> 0, of which waited for: 5 -> 0; matrix products, arithmetic and copies ran while one was open for 0% -> 0% of each run, Pallas kernels for 0% -> 0%
where the time goes in v1:
time: 211 us
  Pallas kernels  207 us (98%)
  local copies, waits for them, and re-layouts  2.89 us (1%)
    pallas_call x1, Pallas kernels, local(): pl.pallas_call(functools.partial(kernel, n, count, tiles), out_shape=(jax...  207 us

profile of v1, /device:TPU:1, one launch (start us, length us, event | category | flops | bytes accessed | tf_op | source)
XLA Modules:
  0.0 210.7 jit_solution(7649532942500911554)
XLA Ops:
  0.6 207.1 %lm_step.1 = (f32[14,16384]{1,0:T(8,128)}, f32[32,256]{1,0:T(8,128)}) custom-call(f32[14,16384]{1,0:T(8,128)} %par.1, f32[416,256]{1,0:T(8,128)} %bitcast.6, s32[2,32]{1,0:T(2,128)} %bitcast.7, s32[2,32]{1,0:T(2,128)} %bitcast.8, s32[32,32]{1,0:T(8,128)} %rank.1, f32[32,256]{1,0:T(8,128)} %target.1), custom_call_target="tpu_custom_call" | custom-call | tf_op jit(solution)/shard_map/lm_step/pallas_call | solution.py:415
  207.8 0.0 copy-start
  207.8 2.3 %copy.9 = f32[14,16384]{1,0:T(8,128)} copy(f32[14,16384]{1,0:T(8,128)} %get-tuple-element.4) | data formatting | bytes 1835008
  210.0 0.0 copy-done
  210.0 0.6 copy.10
Async XLA Ops:
  207.8 2.3 %copy-start = (f32[32,256]{1,0:T(8,128)S(1)}, f32[32,256]{1,0:T(8,128)}, u32[]{:S(2)}) copy-start(f32[32,256]{1,0:T(8,128)} %get-tuple-element.5) | copy-start | bytes 98308

commit v2 on v1

v2 whole, which is shorter than its diff:
```python
import functools

import jax
import jax.numpy as jnp
from jax import lax
from jax.experimental import pallas as pl
from jax.experimental.pallas import tpu as pltpu
from jax.sharding import PartitionSpec as P

MESH = pl.DeviceIdType.MESH
ALPHA = 0.004
DAMPING = 0.1
RIDGE = 0.0001
ITERS = 3
SIDE = 4
SEMS = 128
G = 128
CP = 16
f32 = jnp.float32
bf16 = jnp.bfloat16
NT = (((1,), (1,)), ((), ()))
TN = (((0,), (0,)), ((), ()))


def split2(x):
    hi = x.astype(bf16)
    return hi, (x - hi.astype(f32)).astype(bf16)


def split3(x):
    hi = x.astype(bf16)
    rest = x - hi.astype(f32)
    mid = rest.astype(bf16)
    return hi, mid, (rest - mid.astype(f32)).astype(bf16)


def dot(a, b, dims=(((1,), (0,)), ((), ()))):
    return lax.dot_general(a, b, dims, preferred_element_type=f32)


def lanes(ref, row):
    return jnp.concatenate([ref[pl.ds(row, 1), :], ref[pl.ds(row + 1, 1), :]], axis=1)


def kernel(
    n, params, tiles,
    par, basis, ids, ids_rows, rank, target,
    step, residual,
    b16, bst, S, W, hi, lo, stk, onehot,
    bl_out, bl_in, fr_out, fr_in,
    u_out, u_pair, u_z, u_now, tally_out, tally_in,
    w_out, part_a, part_b, half_a, half_b, last_a, last_b,
    z, direction, total_step, z_flat, z_shard, shard, dot_in,
    sems,
):
    view = lax.axis_index("view")
    scene = lax.axis_index("scene")
    y, x = view // SIDE, lax.rem(view, SIDE)
    zz, core = scene // 2, lax.rem(scene, 2)
    partner = (view, scene + 1 - 2 * core)
    barrier = pltpu.get_barrier_semaphore()

    def greet(d, c):
        pl.semaphore_signal(barrier, inc=1, device_id=(lax.rem(view + d, n), scene), device_id_type=MESH)
        pl.semaphore_signal(barrier, inc=1, device_id=(lax.rem(view + d, n), scene + 1 - 2 * core), device_id_type=MESH)
        pl.semaphore_signal(barrier, inc=1, device_id=(view, lax.rem(scene + d, n)), device_id_type=MESH)
        return c

    lax.fori_loop(1, n, greet, 0)
    counter = iter(range(SEMS))
    new_sem = lambda: sems.at[next(counter)]

    def push(src, dst, send_sem, recv_sem, where):
        pltpu.make_async_remote_copy(
            src_ref=src, dst_ref=dst, send_sem=send_sem, recv_sem=recv_sem, device_id=where, device_id_type=MESH,
        ).start()

    def wait(ref, sem):
        pltpu.make_async_copy(ref, ref, sem).wait()

    def to_scene(src_of, dst, send_sem, recv_sem):
        def body(d, c):
            peer = lax.rem(scene + d, n)
            push(src_of(peer), dst, send_sem, recv_sem, (view, peer))
            return c

        lax.fori_loop(1, n, body, 0)

    block_at = lax.broadcasted_iota(jnp.int32, (G, tiles), 0)
    hot = [jnp.where(block_at == ids_rows[pl.ds(j, 1), :], 1.0, 0.0).astype(bf16) for j in range(2)]
    onehot[...] = jnp.concatenate(hot + hot, axis=1)
    below = lax.broadcasted_iota(jnp.int32, (G, G), 1) < lax.broadcasted_iota(jnp.int32, (G, G), 0)
    below = jnp.where(below, 1.0, 0.0).astype(bf16)
    below = jnp.concatenate([below, below], axis=1)

    halves = [w_out.at[h].reshape(n * (params + 1) * 8, G) for h in range(2)]
    for h in range(2):
        halves[h][pl.ds(0, (params - 1) * tiles)] = basis[:, G * h : G * (h + 1)]

    def prepare(t, c):
        full = jnp.concatenate([half[pl.ds(t, params - 1, stride=tiles), :] for half in halves], axis=1)
        full = jnp.concatenate([full, jnp.zeros((CP - params + 1, full.shape[1]), f32)], axis=0)
        b16[t] = full
        bh, bl = split2(full)
        bst[t] = jnp.concatenate([bh, bh, bl], axis=0)
        return c

    lax.fori_loop(0, tiles, prepare, 0)

    def stage(b, c):
        piece = par[:, pl.ds(pl.multiple_of(b * G, G), G)]
        direction[b] = jnp.concatenate([piece, jnp.zeros((CP - params, G), f32)], axis=0)
        return c

    lax.fori_loop(0, G, stage, 0, unroll=4)
    z_flat[8 * (params + 1) :] = jnp.zeros((8 * (CP - params - 1), G), f32)

    def listing_params(t, j):
        return direction[ids[j, t]]

    def slot_row(t, j):
        return 8 * (t // 2) + 4 * j + 2 * lax.rem(t, 2)

    def opacities(t, c):
        bh, bm, bl = split3(b16[t])
        rhs = jnp.concatenate([bh, bm, bh, bl, bh, bm], axis=0)
        for j in range(2):
            p = 2 * t + j
            vh, vm, vl = split3(listing_params(t, j))
            lhs = jnp.concatenate([vh, vh, vm, vh, vl, vm], axis=0)
            logit = dot(lhs, rhs, TN)
            o = ALPHA * (1.0 / (1.0 + jnp.exp(-logit)))
            keep = -o * (1.0 + o * (0.5 + o * (1.0 / 3.0 + o * 0.25)))
            W[p] = o
            kh, kl = split2(keep)
            hi[p, :, :256] = kh
            lo[p, :, :256] = kl
            total = jnp.sum(keep, axis=0, keepdims=True)
            r = slot_row(t, j)
            bl_out[pl.ds(r, 1), :] = total[:, :G]
            bl_out[pl.ds(r + 1, 1), :] = total[:, G:]
        return c

    lax.fori_loop(0, tiles, opacities, 0, unroll=2)

    pl.semaphore_wait(barrier, 3 * (n - 1))
    rows8 = lambda ref, i: ref.at[pl.ds(pl.multiple_of(i * 8, 8), 8)]
    some8 = lambda ref: ref.at[pl.ds(0, 8 * (n - 1))]
    front_sems = [new_sem() for _ in range(4)]
    to_scene(lambda peer: rows8(bl_out, peer), rows8(bl_in, scene), front_sems[0], front_sems[1])
    rows8(bl_in, scene)[...] = rows8(bl_out, scene)[...]

    def weights(t, c):
        for j in range(2):
            p = 2 * t + j
            keeps = jnp.concatenate([hi[p, :, :256], lo[p, :, :256]], axis=0)
            inner = dot(below, keeps)
            o = W[p]
            colour = jnp.transpose(listing_params(t, j))[:, params - 1 : params]
            w = jnp.exp(inner) * o
            W[p] = w
            S[p] = w * colour * (1.0 - o * (1.0 / ALPHA))
        return c

    lax.fori_loop(0, tiles // 2, weights, 0)

    wait(some8(bl_in), front_sems[1])
    wait(some8(bl_out), front_sems[0])
    slots = 2 * n
    eye = lax.broadcasted_iota(jnp.int32, (slots, slots), 0) == lax.broadcasted_iota(jnp.int32, (slots, slots), 1)
    for i in range(2):
        rank_row = jnp.broadcast_to(rank[pl.ds(2 * scene + i, 1), :].astype(f32), (slots, slots))
        rank_col = jnp.sum(jnp.where(eye, rank_row, 0.0), axis=1, keepdims=True)
        earlier = jnp.where(rank_row < rank_col, 1.0, 0.0).astype(bf16)
        for h in range(2):
            lh, lm, ll = split3(bl_in[pl.ds(2 * i + h, slots, stride=4), :])
            front = dot(earlier, lh) + dot(earlier, lm) + dot(earlier, ll)
            fr_out[pl.ds(2 * i + h, slots, stride=4), :] = jnp.exp(front)
    to_scene(lambda peer: rows8(fr_out, peer), rows8(fr_in, scene), front_sems[2], front_sems[3])
    rows8(fr_in, scene)[...] = rows8(fr_out, scene)[...]

    lax.fori_loop(tiles // 2, tiles, weights, 0)
    wait(some8(fr_in), front_sems[3])
    wait(some8(fr_out), front_sems[2])

    def put_u(t, value):
        u_out[pl.ds(2 * t, 1), :] = value[:, :G]
        u_out[pl.ds(2 * t + 1, 1), :] = value[:, G:]

    mine, other = core * (tiles // 2), (1 - core) * (tiles // 2)

    def half_loop(first, body, unroll):
        def step_of(i, c):
            body(first + i)
            return c

        lax.fori_loop(0, tiles // 2, step_of, 0, unroll=unroll)

    def finish(t):
        total = jnp.zeros((1, 2 * G), f32)
        for j in range(2):
            p = 2 * t + j
            factor = lanes(fr_in, slot_row(t, j))
            w = W[p] * factor
            s = S[p] * factor
            W[p] = w
            S[p] = s
            sh, sl = split2(s)
            wh, wl = split2(w)
            hi[p, :, :256] = sh
            hi[p, :, 256:] = wh
            lo[p, :, :256] = sl
            lo[p, :, 256:] = wl
            colour = jnp.transpose(listing_params(t, j))[:, params - 1 : params]
            total = total + jnp.sum(w * colour, axis=0, keepdims=True)
        put_u(t, total)

    half_rows = lambda ref, first: ref.at[pl.ds(pl.multiple_of(2 * first, 8), tiles)]

    class SceneSum:
        def __init__(self, q):
            self.q, self.sems = q, [new_sem() for _ in range(6)]

        def run(self, body, unroll):
            q, sem = self.q, self.sems
            half_loop(other, body, unroll)
            push(half_rows(u_out, other), u_pair.at[q], sem[0], sem[1], partner)
            half_loop(mine, body, unroll)
            wait(u_pair.at[q], sem[1])
            u_z[q, zz] = half_rows(u_out, mine)[...] + u_pair[q]
            for d in (4, 3, 5, 2, 6, 1, 7):
                push(u_z.at[q, zz], u_z.at[q, zz], sem[2], sem[3], (view, lax.rem(scene + 2 * d, n)))
            wait(u_pair.at[q], sem[0])

        def total(self):
            q, sem = self.q, self.sems
            wait(u_z.at[q, pl.ds(0, n // 2 - 1)], sem[3])
            wait(u_z.at[q, pl.ds(0, n // 2 - 1)], sem[2])
            out = u_z[q, 0]
            for i in range(1, n // 2):
                out = out + u_z[q, i]
            return out

        def publish(self, value):
            q, sem = self.q, self.sems
            rows = half_rows(u_now.at[q], mine)
            rows[...] = value
            push(rows, rows, sem[4], sem[5], partner)

        def rest(self):
            q, sem = self.q, self.sems
            wait(half_rows(u_now.at[q], other), sem[5])
            wait(half_rows(u_now.at[q], other), sem[4])

    render = SceneSum(0)
    render.run(finish, 2)

    def scatter_blocks(slot):
        for c in range(0, params, 2):
            x = jnp.concatenate([stk[pl.ds((c + e) * 2 * tiles, 2 * tiles), :] for e in range(2)], axis=1)
            xh, xl = split2(x)
            out = dot(onehot[...], jnp.concatenate([xh, xl], axis=0))
            w_out[slot, :, c] = out[:, :G].reshape(n, 8, G)
            w_out[slot, :, c + 1] = out[:, G:].reshape(n, 8, G)

    def put_listing(t, value):
        for j in range(2):
            stk[pl.ds(tiles * j + t, CP, stride=2 * tiles), :] = value[:, G * j : G * (j + 1)]

    row_a, row_b = pl.ds(0, 8), pl.ds(8, params - 7)

    class ViewScatter:
        def __init__(self, q, slot):
            self.q, self.slot = q, slot
            self.send_sem, self.last = new_sem(), [new_sem(), new_sem()]
            self.first = [[new_sem() for _ in range(SIDE)] for _ in range(2)]

        def start(self):
            q, slot = self.q, self.slot
            for e in (2, 1, 3, 0):
                for d in (2, 1, 3):
                    to_x, to_y = lax.rem(x + d, SIDE), lax.rem(y + d, SIDE)
                    line_y, line_x = lax.rem(y + e, SIDE), lax.rem(x + e, SIDE)
                    push(w_out.at[slot, line_y * SIDE + to_x, row_a], part_a.at[q, d - 1, line_y],
                         self.send_sem, self.first[0][e], (y * SIDE + to_x, scene))
                    push(w_out.at[slot, to_y * SIDE + line_x, row_b], part_b.at[q, d - 1, line_x],
                         self.send_sem, self.first[1][e], (to_y * SIDE + x, scene))

        def middle(self):
            q, slot = self.q, self.slot
            for e in (2, 1, 3, 0):
                line_y, line_x = lax.rem(y + e, SIDE), lax.rem(x + e, SIDE)
                wait(part_a.at[q, :, line_y], self.first[0][e])
                total = w_out[slot, line_y * SIDE + x, row_a] + part_a[q, 0, line_y]
                half_a[q, line_y] = total + part_a[q, 1, line_y] + part_a[q, 2, line_y]
                if e:
                    push(half_a.at[q, line_y], last_a.at[q, e - 1], self.send_sem, self.last[0], (line_y * SIDE + x, scene))
                wait(part_b.at[q, :, line_x], self.first[1][e])
                total = w_out[slot, y * SIDE + line_x, row_b] + part_b[q, 0, line_x]
                half_b[q, line_x] = total + part_b[q, 1, line_x] + part_b[q, 2, line_x]
                if e:
                    push(half_b.at[q, line_x], last_b.at[q, e - 1], self.send_sem, self.last[1], (y * SIDE + line_x, scene))

        def total(self):
            q, slot = self.q, self.slot
            wait(last_a.at[q], self.last[0])
            wait(last_b.at[q], self.last[1])
            wait(w_out.at[slot, pl.ds(0, n - 1)], self.send_sem)
            out_a, out_b = half_a[q, y], half_b[q, x]
            for d in range(SIDE - 1):
                out_a, out_b = out_a + last_a[q, d], out_b + last_b[q, d]
            return jnp.concatenate([out_a, out_b], axis=0)

    is_colour = lax.broadcasted_iota(jnp.int32, (CP, 256), 0) == params - 1

    def transpose_rows(left_s, left_w, right_hi, right_lo):
        sh, sl = split2(left_s)
        wh, wl = split2(left_w)
        high = jnp.concatenate([sh, wh], axis=1)
        both = jnp.concatenate([high, jnp.concatenate([sl, wl], axis=1)], axis=0)
        first = dot(both, right_hi, NT)
        return first[:CP] + first[CP:] + dot(high, right_lo, NT)

    def diagonal(t, c):
        left_s = b16[t] * b16[t]
        left_w = jnp.where(is_colour, 1.0, 0.0)
        parts = []
        for j in range(2):
            p = 2 * t + j
            sh, sl = split2(S[p] * S[p])
            wh, wl = split2(W[p] * W[p])
            parts.append(transpose_rows(
                left_s, left_w, jnp.concatenate([sh, wh], axis=1), jnp.concatenate([sl, wl], axis=1)))
        put_listing(t, jnp.concatenate(parts, axis=1))
        return c

    lax.fori_loop(0, tiles, diagonal, 0, unroll=2)
    scatter_blocks(0)
    w_out[0, :, params] = jnp.zeros((n, 8, G), f32)
    diag_sum = ViewScatter(0, 0)
    diag_sum.start()
    render.publish(render.total())

    def apply_transpose(t, u):
        left_s = b16[t] * u
        left_w = jnp.where(is_colour, u, 0.0)
        right_hi = jnp.concatenate([hi[2 * t], hi[2 * t + 1]], axis=0)
        right_lo = jnp.concatenate([lo[2 * t], lo[2 * t + 1]], axis=0)
        put_listing(t, transpose_rows(left_s, left_w, right_hi, right_lo))

    def gradient(t):
        u = lanes(u_now.at[0], 2 * t) - target[pl.ds(t, 1), :]
        residual[pl.ds(t, 1), :] = u
        apply_transpose(t, u)

    half_loop(mine, gradient, 4)
    diag_sum.middle()
    render.rest()
    half_loop(other, gradient, 4)
    scatter_blocks(1)
    w_out[1, :, params] = jnp.zeros((n, 8, G), f32)
    grad_sum = ViewScatter(1, 1)
    grad_sum.start()

    R, Z, DP, D = 0, 1, 2, 3

    def lane_sum(x):
        return jnp.sum(x, axis=1, keepdims=True)

    shard[D] = diag_sum.total()[:params]
    grad_sum.middle()
    shard[R] = -grad_sum.total()[:params]

    def gather_z(k):
        d = shard[D]
        r = shard[R]
        zs = r / ((1.0 + DAMPING) * d + RIDGE)
        dz = (DAMPING * d + RIDGE) * zs
        part = lambda x: jnp.sum(jnp.sum(x, axis=0), axis=0, keepdims=True)
        rows = [part(r * zs), part(zs * dz)]
        rows.append(part(shard[Z] * dz) if k else jnp.zeros((1, G), f32))
        rows.append(jnp.zeros((5, G), f32))
        z_flat[pl.ds(0, 8 * params)] = zs.reshape(8 * params, G)
        z_flat[pl.ds(8 * params, 8)] = jnp.concatenate(rows, axis=0)
        for i in range(8):
            z_shard[k, i] = z_flat[pl.ds(i, CP, stride=8), :]
        rows8(z.at[k], view)[...] = z_shard[k]
        rest_sem, send_sem = new_sem(), new_sem()
        sem_a, sem_b = [None] + [new_sem() for _ in range(3)], [None] + [new_sem() for _ in range(3)]
        line = z.at[k]
        part_of = lambda owner, h: line.at[pl.ds(pl.multiple_of(8 * owner + 4 * h, 4), 4)]
        own = [z_shard.at[k, pl.ds(4 * h, 4)] for h in range(2)]
        at_x = lambda d: (y * SIDE + lax.rem(x + d, SIDE), scene)
        at_y = lambda d: (lax.rem(y + d, SIDE) * SIDE + x, scene)
        for d in (1, 3, 2):
            push(own[0], part_of(view, 0), send_sem, sem_a[d], at_x(d))
            push(own[1], part_of(view, 1), send_sem, sem_b[d], at_y(d))
        for d in (1, 3, 2):
            push(own[1], part_of(view, 1), send_sem, rest_sem, at_x(d))
            push(own[0], part_of(view, 0), send_sem, rest_sem, at_y(d))
        for d in (1, 3, 2):
            from_x = y * SIDE + lax.rem(x + SIDE - d, SIDE)
            from_y = lax.rem(y + SIDE - d, SIDE) * SIDE + x
            wait(part_of(from_x, 0), sem_a[d])
            for e in (2, 1, 3):
                push(part_of(from_x, 0), part_of(from_x, 0), send_sem, rest_sem, at_y(e))
            wait(part_of(from_y, 1), sem_b[d])
            for e in (2, 1, 3):
                push(part_of(from_y, 1), part_of(from_y, 1), send_sem, rest_sem, at_x(e))
        wait(line.at[pl.ds(0, 4 * 24)], rest_sem)
        wait(line.at[pl.ds(0, 4 * 30)], send_sem)
        return zs

    one = jnp.ones((1, 1), f32)
    rz_old, pdp = one, 0.0 * one
    for k in range(ITERS):
        zs = gather_z(k)
        flat = z.at[k].reshape(CP * G, G)
        sums = [
            jnp.sum(flat[pl.ds(CP * i + params, n, stride=8 * CP), :], axis=0, keepdims=True) for i in range(3)]
        tally_out[k] = jnp.concatenate(sums + [jnp.zeros((5, G), f32)], axis=0)
        tally_sems = [new_sem(), new_sem()]
        rows8(tally_in.at[k], scene)[...] = tally_out[k]
        to_scene(lambda peer: tally_out.at[k], rows8(tally_in.at[k], scene), *tally_sems)

        def forward(t):
            v = jnp.concatenate(
                [z[k, ids[j, t]] for j in range(2)], axis=1)
            vh, vl = split2(v)
            lhs = jnp.concatenate([vh, vl, vh], axis=0)
            total = jnp.zeros((1, 2 * G), f32)
            for j in range(2):
                p = 2 * t + j
                projected = dot(lhs[:, G * j : G * (j + 1)], bst[t], TN)
                tint = jnp.transpose(v[:, G * j : G * (j + 1)])[:, params - 1 : params]
                total = total + jnp.sum(S[p] * projected + W[p] * tint, axis=0, keepdims=True)
            put_u(t, total)

        product = SceneSum(k + 1)
        product.run(forward, 4)
        wait(some8(tally_in.at[k]), tally_sems[1])
        wait(some8(tally_in.at[k]), tally_sems[0])
        tally = tally_in[k, pl.ds(0, 8), :]
        for i in range(1, n):
            tally = tally + tally_in[k, pl.ds(8 * i, 8), :]
        totals = lane_sum(tally)
        rz, zdz, zdp = totals[0:1], totals[1:2], totals[2:3]
        beta = rz / rz_old if k else 0.0 * one
        u = product.total()
        if k:
            u = u + beta * half_rows(u_now.at[k], mine)[...]
        if k + 1 < ITERS:
            product.publish(u)
        pdp = zdz + 2.0 * beta * zdp + beta * beta * pdp
        if k:
            direction[...] = z[k] + beta * direction[...]
            shard[Z] = zs + beta * shard[Z]
        else:
            direction[...] = z[k]
            shard[Z] = zs
        if k + 1 < ITERS:
            back = lambda t: apply_transpose(t, lanes(u_now.at[k + 1], 2 * t))
            half_loop(mine, back, 4)
            product.rest()
            half_loop(other, back, 4)
            scatter_blocks(k)
            square = jnp.sum(u_now[k + 1] * u_now[k + 1], axis=0, keepdims=True)
            w_out[k, :, params] = jnp.broadcast_to(square, (n, 8, G))
            image_sum = ViewScatter(k + 2, k)
            image_sum.start()
            image_sum.middle()
            w = image_sum.total()
            a = rz / (lane_sum(w[params, 0:1]) + pdp)
            image = w[:params] + (DAMPING * shard[D] + RIDGE) * shard[Z]
            shard[R] = shard[R] - a * image
        else:
            squares = rows8(dot_in, 2 * view + core)
            squares[...] = jnp.broadcast_to(jnp.sum(u * u, axis=0, keepdims=True), (8, G))
            dot_sems = [new_sem(), new_sem()]

            def share(d, c):
                there = lax.rem(view + d, n)
                push(squares, squares, *dot_sems, (there, scene))
                push(squares, squares, *dot_sems, (there, scene + 1 - 2 * core))
                return c

            push(squares, squares, *dot_sems, partner)
            lax.fori_loop(1, n, share, 0)
            wait(dot_in.at[pl.ds(0, 8 * (2 * n - 1))], dot_sems[1])
            wait(dot_in.at[pl.ds(0, 8 * (2 * n - 1))], dot_sems[0])
            total = dot_in[pl.ds(0, 8), :]
            for i in range(1, 2 * n):
                total = total + dot_in[pl.ds(8 * i, 8), :]
            a = rz / (lane_sum(total[0:1]) + pdp)
        if k + 1 == ITERS:
            for b in range(G):
                step[:, pl.ds(b * G, G)] = (total_step[b] + a * direction[b])[:params]
        elif k:
            total_step[...] = total_step[...] + a * direction[...]
        else:
            total_step[...] = a * direction[...]
        rz_old = rz


def local(n, params, pixel_basis, tile_blocks, depth_rank, target):
    count = params.shape[0]
    tiles, _, pixels = pixel_basis.shape
    ids = tile_blocks.transpose(1, 2, 0).reshape(2, tiles)
    basis = pixel_basis.transpose(1, 0, 2).reshape((count - 1) * tiles, pixels)
    vmem = pl.BlockSpec(memory_space=pltpu.VMEM)
    lists = 2 * tiles
    return pl.pallas_call(
        functools.partial(kernel, n, count, tiles),
        out_shape=(
            jax.ShapeDtypeStruct((count, G * G), f32),
            jax.ShapeDtypeStruct((tiles, pixels), f32),
        ),
        in_specs=[vmem, vmem, pl.BlockSpec(memory_space=pltpu.SMEM), vmem, vmem, vmem],
        out_specs=(vmem, vmem),
        scratch_shapes=[
            pltpu.VMEM((tiles, CP, pixels), f32),
            pltpu.VMEM((tiles, 3 * CP, pixels), bf16),
            pltpu.VMEM((lists, G, pixels), f32),
            pltpu.VMEM((lists, G, pixels), f32),
            pltpu.VMEM((lists, G, 2 * pixels), bf16),
            pltpu.VMEM((lists, G, 2 * pixels), bf16),
            pltpu.VMEM((CP * lists, G), f32),
            pltpu.VMEM((G, 2 * lists), bf16),
            pltpu.VMEM((8 * n, G), f32),
            pltpu.VMEM((8 * n, G), f32),
            pltpu.VMEM((8 * n, G), f32),
            pltpu.VMEM((8 * n, G), f32),
            pltpu.VMEM((2 * tiles, G), f32),
            pltpu.VMEM((ITERS + 1, tiles, G), f32),
            pltpu.VMEM((ITERS + 1, n // 2, tiles, G), f32),
            pltpu.VMEM((ITERS + 1, 2 * tiles, G), f32),
            pltpu.VMEM((ITERS, 8, G), f32),
            pltpu.VMEM((ITERS, 8 * n, G), f32),
            pltpu.VMEM((2, n, count + 1, 8, G), f32),
            pltpu.VMEM((ITERS + 1, SIDE - 1, SIDE, 8, 8, G), f32),
            pltpu.VMEM((ITERS + 1, SIDE - 1, SIDE, count - 7, 8, G), f32),
            pltpu.VMEM((ITERS + 1, SIDE, 8, 8, G), f32),
            pltpu.VMEM((ITERS + 1, SIDE, count - 7, 8, G), f32),
            pltpu.VMEM((ITERS + 1, SIDE - 1, 8, 8, G), f32),
            pltpu.VMEM((ITERS + 1, SIDE - 1, count - 7, 8, G), f32),
            pltpu.VMEM((ITERS, G, CP, G), f32),
            pltpu.VMEM((G, CP, G), f32),
            pltpu.VMEM((G, CP, G), f32),
            pltpu.VMEM((8 * CP, G), f32),
            pltpu.VMEM((ITERS, 8, CP, G), f32),
            pltpu.VMEM((4, count, 8, G), f32),
            pltpu.VMEM((16 * n, G), f32),
            pltpu.SemaphoreType.DMA((SEMS,)),
        ],
        compiler_params=pltpu.CompilerParams(
            collective_id=0, has_side_effects=True, vmem_limit_bytes=64 * 1024 * 1024 - 65536),
        name="lm_step",
    )(params, basis, ids, ids, depth_rank, target)


def solution(mesh):
    in_specs = (
        P(None, "scene"),
        P("view", None, None),
        P("view", "scene", None),
        P("view", None),
        P("view", None),
    )
    out_specs = (P(None, "scene"), P("view", None))
    step = functools.partial(local, mesh.shape["scene"])
    return jax.shard_map(step, mesh=mesh, in_specs=in_specs, out_specs=out_specs, check_vma=False)
```

time: 211 us -> 166 us (0.79)
  Pallas kernels: 207 us -> 162 us
    pallas_call x1, Pallas kernels: 207 us -> 162 us  [local(): pl.pallas_call(functools.partial(kernel, n, count, tiles), out_shape=(jax...]
where the time goes in v2:
time: 166 us
  Pallas kernels  162 us (98%)
  local copies, waits for them, and re-layouts  2.89 us (2%)
    pallas_call x1, Pallas kernels, local(): pl.pallas_call(functools.partial(kernel, n, count, tiles), out_shape=(jax...  162 us

profile of v2, /device:TPU:1, one launch (start us, length us, event | category | flops | bytes accessed | tf_op | source)
XLA Modules:
  0.0 165.7 jit_solution(2832034542378913578)
XLA Ops:
  0.6 162.1 %lm_step.1 = (f32[14,16384]{1,0:T(8,128)}, f32[32,256]{1,0:T(8,128)}) custom-call(f32[14,16384]{1,0:T(8,128)} %par.1, f32[416,256]{1,0:T(8,128)} %bitcast.6, s32[2,32]{1,0:T(2,128)} %bitcast.7, s32[2,32]{1,0:T(2,128)} %bitcast.8, s32[32,32]{1,0:T(8,128)} %rank.1, f32[32,256]{1,0:T(8,128)} %target.1), custom_call_target="tpu_custom_call" | custom-call | tf_op jit(solution)/shard_map/lm_step/pallas_call | solution.py:512
  162.8 0.0 copy-start
  162.8 2.3 %copy.9 = f32[14,16384]{1,0:T(8,128)} copy(f32[14,16384]{1,0:T(8,128)} %get-tuple-element.4) | data formatting | bytes 1835008
  165.1 0.0 copy-done
  165.1 0.6 copy.10
Async XLA Ops:
  162.8 2.3 %copy-start = (f32[32,256]{1,0:T(8,128)S(1)}, f32[32,256]{1,0:T(8,128)}, u32[]{:S(2)}) copy-start(f32[32,256]{1,0:T(8,128)} %get-tuple-element.5) | copy-start | bytes 98308

commit v3 on v2

v3 whole, which is shorter than its diff:
```python
import functools

import jax
import jax.numpy as jnp
from jax import lax
from jax.experimental import pallas as pl
from jax.experimental.pallas import tpu as pltpu
from jax.sharding import PartitionSpec as P

MESH = pl.DeviceIdType.MESH
ALPHA = 0.004
DAMPING = 0.1
RIDGE = 0.0001
ITERS = 3
SIDE = 4
SEMS = 224
PARTS = ((0, 4, 8), (8, 11, 14))
G = 128
CP = 16
f32 = jnp.float32
bf16 = jnp.bfloat16
NT = (((1,), (1,)), ((), ()))
TN = (((0,), (0,)), ((), ()))


def split2(x):
    hi = x.astype(bf16)
    return hi, (x - hi.astype(f32)).astype(bf16)


def split3(x):
    hi = x.astype(bf16)
    rest = x - hi.astype(f32)
    mid = rest.astype(bf16)
    return hi, mid, (rest - mid.astype(f32)).astype(bf16)


def dot(a, b, dims=(((1,), (0,)), ((), ()))):
    return lax.dot_general(a, b, dims, preferred_element_type=f32)


def lanes(ref, row):
    return jnp.concatenate([ref[pl.ds(row, 1), :], ref[pl.ds(row + 1, 1), :]], axis=1)


def kernel(
    n, params, tiles,
    par, basis, ids, ids_rows, rank, target,
    base, last_direction, scale, residual,
    b16, bst, S, W, hi, lo, stk, onehot,
    bl_out, bl_in, fr_out, fr_in,
    u_out, u_pair, u_z, u_now, tally_out, tally_in,
    w_out, parts, half, last,
    z, z_in, direction, total_step, z_shard, shard, dot_in,
    sems,
):
    view = lax.axis_index("view")
    scene = lax.axis_index("scene")
    y, x = view // SIDE, lax.rem(view, SIDE)
    zz, core = scene // 2, lax.rem(scene, 2)
    partner = (view, scene + 1 - 2 * core)
    barrier = pltpu.get_barrier_semaphore()

    def greet(d, c):
        pl.semaphore_signal(barrier, inc=1, device_id=(lax.rem(view + d, n), scene), device_id_type=MESH)
        pl.semaphore_signal(barrier, inc=1, device_id=(lax.rem(view + d, n), scene + 1 - 2 * core), device_id_type=MESH)
        pl.semaphore_signal(barrier, inc=1, device_id=(view, lax.rem(scene + d, n)), device_id_type=MESH)
        return c

    lax.fori_loop(1, n, greet, 0)
    counter = iter(range(SEMS))
    new_sem = lambda: sems.at[next(counter)]

    def push(src, dst, send_sem, recv_sem, where):
        pltpu.make_async_remote_copy(
            src_ref=src, dst_ref=dst, send_sem=send_sem, recv_sem=recv_sem, device_id=where, device_id_type=MESH,
        ).start()

    def wait(ref, sem):
        pltpu.make_async_copy(ref, ref, sem).wait()

    def to_scene(src_of, dst, send_sem, recv_sem):
        def body(d, c):
            peer = lax.rem(scene + d, n)
            push(src_of(peer), dst, send_sem, recv_sem, (view, peer))
            return c

        lax.fori_loop(1, n, body, 0)

    block_at = lax.broadcasted_iota(jnp.int32, (G, tiles), 0)
    hot = [jnp.where(block_at == ids_rows[pl.ds(j, 1), :], 1.0, 0.0).astype(bf16) for j in range(2)]
    onehot[...] = jnp.concatenate(hot + hot, axis=1)
    below = lax.broadcasted_iota(jnp.int32, (G, G), 1) < lax.broadcasted_iota(jnp.int32, (G, G), 0)
    below = jnp.where(below, 1.0, 0.0).astype(bf16)
    below = jnp.concatenate([below, below], axis=1)

    halves = [w_out.at[h].reshape(n * params * 8, G) for h in range(2)]
    for h in range(2):
        halves[h][pl.ds(0, (params - 1) * tiles)] = basis[:, G * h : G * (h + 1)]

    def prepare(t, c):
        full = jnp.concatenate([half[pl.ds(t, params - 1, stride=tiles), :] for half in halves], axis=1)
        full = jnp.concatenate([full, jnp.zeros((CP - params + 1, full.shape[1]), f32)], axis=0)
        b16[t] = full
        bh, bl = split2(full)
        bst[t] = jnp.concatenate([bh, bh, bl], axis=0)
        return c

    lax.fori_loop(0, tiles, prepare, 0, unroll=4)

    def stage(b, c):
        piece = par[:, pl.ds(pl.multiple_of(b * G, G), G)]
        direction[b] = jnp.concatenate([piece, jnp.zeros((CP - params, G), f32)], axis=0)
        return c

    lax.fori_loop(0, G, stage, 0, unroll=8)
    z[:, params + 1 :] = jnp.zeros((G, CP - params - 1, G), f32)

    def listing_params(t, j):
        return direction[ids[j, t]]

    def slot_row(t, j):
        return 8 * (t // 2) + 4 * j + 2 * lax.rem(t, 2)

    def opacities(t, c):
        bh, bm, bl = split3(b16[t])
        rhs = jnp.concatenate([bh, bm, bh, bl, bh, bm], axis=0)
        for j in range(2):
            p = 2 * t + j
            vh, vm, vl = split3(listing_params(t, j))
            lhs = jnp.concatenate([vh, vh, vm, vh, vl, vm], axis=0)
            logit = dot(lhs, rhs, TN)
            o = ALPHA * (1.0 / (1.0 + jnp.exp(-logit)))
            keep = -o * (1.0 + o * (0.5 + o * (1.0 / 3.0 + o * 0.25)))
            W[p] = o
            kh, kl = split2(keep)
            hi[p] = kh
            lo[p] = kl
            total = jnp.sum(keep, axis=0, keepdims=True)
            r = slot_row(t, j)
            bl_out[pl.ds(r, 1), :] = total[:, :G]
            bl_out[pl.ds(r + 1, 1), :] = total[:, G:]
        return c

    lax.fori_loop(0, tiles, opacities, 0, unroll=4)

    pl.semaphore_wait(barrier, 3 * (n - 1))
    rows8 = lambda ref, i: ref.at[pl.ds(pl.multiple_of(i * 8, 8), 8)]
    some8 = lambda ref: ref.at[pl.ds(0, 8 * (n - 1))]
    front_sems = [new_sem() for _ in range(4)]
    to_scene(lambda peer: rows8(bl_out, peer), rows8(bl_in, scene), front_sems[0], front_sems[1])
    rows8(bl_in, scene)[...] = rows8(bl_out, scene)[...]

    def weights(t, c):
        for j in range(2):
            p = 2 * t + j
            keeps = jnp.concatenate([hi[p], lo[p]], axis=0)
            inner = dot(below, keeps)
            o = W[p]
            colour = jnp.transpose(listing_params(t, j))[:, params - 1 : params]
            w = jnp.exp(inner) * o
            W[p] = w
            S[p] = w * colour * (1.0 - o * (1.0 / ALPHA))
        return c

    lax.fori_loop(0, tiles // 2, weights, 0, unroll=4)

    wait(some8(bl_in), front_sems[1])
    wait(some8(bl_out), front_sems[0])
    slots = 2 * n
    eye = lax.broadcasted_iota(jnp.int32, (slots, slots), 0) == lax.broadcasted_iota(jnp.int32, (slots, slots), 1)
    for i in range(2):
        rank_row = jnp.broadcast_to(rank[pl.ds(2 * scene + i, 1), :].astype(f32), (slots, slots))
        rank_col = jnp.sum(jnp.where(eye, rank_row, 0.0), axis=1, keepdims=True)
        earlier = jnp.where(rank_row < rank_col, 1.0, 0.0).astype(bf16)
        for h in range(2):
            lh, lm, ll = split3(bl_in[pl.ds(2 * i + h, slots, stride=4), :])
            front = dot(earlier, lh) + dot(earlier, lm) + dot(earlier, ll)
            fr_out[pl.ds(2 * i + h, slots, stride=4), :] = jnp.exp(front)
    to_scene(lambda peer: rows8(fr_out, peer), rows8(fr_in, scene), front_sems[2], front_sems[3])
    rows8(fr_in, scene)[...] = rows8(fr_out, scene)[...]

    lax.fori_loop(tiles // 2, tiles, weights, 0, unroll=4)
    wait(some8(fr_in), front_sems[3])
    wait(some8(fr_out), front_sems[2])

    def put_u(t, value):
        u_out[pl.ds(2 * t, 1), :] = value[:, :G]
        u_out[pl.ds(2 * t + 1, 1), :] = value[:, G:]

    mine, other = core * (tiles // 2), (1 - core) * (tiles // 2)

    def half_loop(first, body, unroll):
        def step_of(i, c):
            body(first + i)
            return c

        lax.fori_loop(0, tiles // 2, step_of, 0, unroll=unroll)

    def finish(t):
        total = jnp.zeros((1, 2 * G), f32)
        for j in range(2):
            p = 2 * t + j
            factor = lanes(fr_in, slot_row(t, j))
            w = W[p] * factor
            s = S[p] * factor
            W[p] = w
            S[p] = s
            hi[p], lo[p] = split2(s)
            colour = jnp.transpose(listing_params(t, j))[:, params - 1 : params]
            total = total + jnp.sum(w * colour, axis=0, keepdims=True)
        put_u(t, total)

    def rows_of(part, more=0):
        a, b, end = PARTS[part]
        end = end + more * part
        return pl.ds(a, b - a), pl.ds(b, end - b), pl.ds(a, end - a)

    at_x = lambda d: (y * SIDE + lax.rem(x + d, SIDE), scene)
    at_y = lambda d: (lax.rem(y + d, SIDE) * SIDE + x, scene)

    half_rows = lambda ref, first: ref.at[pl.ds(pl.multiple_of(2 * first, 8), tiles)]

    class SceneSum:
        def __init__(self, q):
            self.q, self.sems = q, [new_sem() for _ in range(6)]

        def run(self, body, unroll):
            q, sem = self.q, self.sems
            half_loop(other, body, unroll)
            push(half_rows(u_out, other), u_pair.at[q], sem[0], sem[1], partner)
            half_loop(mine, body, unroll)
            wait(u_pair.at[q], sem[1])
            u_z[q, zz] = half_rows(u_out, mine)[...] + u_pair[q]
            for d in (4, 3, 5, 2, 6, 1, 7):
                push(u_z.at[q, zz], u_z.at[q, zz], sem[2], sem[3], (view, lax.rem(scene + 2 * d, n)))
            wait(u_pair.at[q], sem[0])

        def total(self):
            q, sem = self.q, self.sems
            wait(u_z.at[q, pl.ds(0, n // 2 - 1)], sem[3])
            wait(u_z.at[q, pl.ds(0, n // 2 - 1)], sem[2])
            out = u_z[q, 0]
            for i in range(1, n // 2):
                out = out + u_z[q, i]
            return out

        def publish(self, value):
            q, sem = self.q, self.sems
            rows = half_rows(u_now.at[q], mine)
            rows[...] = value
            push(rows, rows, sem[4], sem[5], partner)

        def rest(self):
            q, sem = self.q, self.sems
            wait(half_rows(u_now.at[q], other), sem[5])
            wait(half_rows(u_now.at[q], other), sem[4])

    render = SceneSum(0)
    render.run(finish, 2)

    def scatter_blocks(slot):
        for c in range(0, params, 2):
            x = jnp.concatenate([stk[pl.ds((c + e) * 2 * tiles, 2 * tiles), :] for e in range(2)], axis=1)
            xh, xl = split2(x)
            out = dot(onehot[...], jnp.concatenate([xh, xl], axis=0))
            w_out[slot, :, c] = out[:, :G].reshape(n, 8, G)
            w_out[slot, :, c + 1] = out[:, G:].reshape(n, 8, G)

    def put_listing(t, value):
        for j in range(2):
            stk[pl.ds(tiles * j + t, CP, stride=2 * tiles), :] = value[:, G * j : G * (j + 1)]

    class ViewScatter:
        def __init__(self, q, slot):
            self.q, self.slot = q, slot
            self.send_sem = [new_sem() for _ in PARTS]
            self.last = [[new_sem(), new_sem()] for _ in PARTS]
            self.first = [[[new_sem() for _ in range(SIDE)] for _ in range(2)] for _ in PARTS]

        def start(self, part):
            q, slot = self.q, self.slot
            row_a, row_b, _ = rows_of(part)
            for e in (2, 1, 3, 0):
                for d in (2, 1, 3):
                    to_x, to_y = lax.rem(x + d, SIDE), lax.rem(y + d, SIDE)
                    line_y, line_x = lax.rem(y + e, SIDE), lax.rem(x + e, SIDE)
                    push(w_out.at[slot, line_y * SIDE + to_x, row_a], parts.at[q, d - 1, line_y, row_a],
                         self.send_sem[part], self.first[part][0][e], (y * SIDE + to_x, scene))
                    push(w_out.at[slot, to_y * SIDE + line_x, row_b], parts.at[q, d - 1, line_x, row_b],
                         self.send_sem[part], self.first[part][1][e], (to_y * SIDE + x, scene))

        def middle(self, part):
            q, slot = self.q, self.slot
            row_a, row_b, _ = rows_of(part)
            for e in (2, 1, 3, 0):
                line_y, line_x = lax.rem(y + e, SIDE), lax.rem(x + e, SIDE)
                for own, line, row, way, to in (
                    (line_y * SIDE + x, line_y, row_a, 0, line_y * SIDE + x),
                    (y * SIDE + line_x, line_x, row_b, 1, y * SIDE + line_x),
                ):
                    wait(parts.at[q, :, line, row], self.first[part][way][e])
                    total = w_out[slot, own, row] + parts[q, 0, line, row]
                    half[q, line, row] = total + parts[q, 1, line, row] + parts[q, 2, line, row]
                    if e:
                        push(half.at[q, line, row], last.at[q, e - 1, row],
                             self.send_sem[part], self.last[part][way], (to, scene))

        def total(self, part):
            q, slot = self.q, self.slot
            row_a, row_b, row = rows_of(part)
            wait(last.at[q, :, row_a], self.last[part][0])
            wait(last.at[q, :, row_b], self.last[part][1])
            wait(w_out.at[slot, pl.ds(0, n - 1), row], self.send_sem[part])
            out_a, out_b = half[q, y, row_a], half[q, x, row_b]
            for d in range(SIDE - 1):
                out_a, out_b = out_a + last[q, d, row_a], out_b + last[q, d, row_b]
            return jnp.concatenate([out_a, out_b], axis=0)

    class ViewGather:
        def __init__(self, k):
            self.k = k
            self.send_sem, self.rest = [new_sem() for _ in PARTS], [new_sem() for _ in PARTS]
            self.near = [[[new_sem() for _ in range(SIDE - 1)] for _ in range(2)] for _ in PARTS]

        def start(self, part):
            k = self.k
            row_a, row_b, row = rows_of(part, 1)
            z_in[k, view, row] = z_shard[k, row]
            src_a, src_b = z_shard.at[k, row_a], z_shard.at[k, row_b]
            dst_a, dst_b = z_in.at[k, view, row_a], z_in.at[k, view, row_b]
            send_sem, rest = self.send_sem[part], self.rest[part]
            for d in (1, 3, 2):
                push(src_a, dst_a, send_sem, self.near[part][0][d - 1], at_x(d))
                push(src_b, dst_b, send_sem, self.near[part][1][d - 1], at_y(d))
            for d in (1, 3, 2):
                push(src_b, dst_b, send_sem, rest, at_x(d))
                push(src_a, dst_a, send_sem, rest, at_y(d))

        def relay(self, part):
            k = self.k
            row_a, row_b, _ = rows_of(part, 1)
            send_sem, rest = self.send_sem[part], self.rest[part]
            for d in (1, 3, 2):
                from_x = y * SIDE + lax.rem(x + SIDE - d, SIDE)
                from_y = lax.rem(y + SIDE - d, SIDE) * SIDE + x
                there_a, there_b = z_in.at[k, from_x, row_a], z_in.at[k, from_y, row_b]
                wait(there_a, self.near[part][0][d - 1])
                for e in (2, 1, 3):
                    push(there_a, there_a, send_sem, rest, at_y(e))
                wait(there_b, self.near[part][1][d - 1])
                for e in (2, 1, 3):
                    push(there_b, there_b, send_sem, rest, at_x(e))

        def finish(self, part):
            k = self.k
            row = rows_of(part, 1)[2]
            wait(z_in.at[k, pl.ds(0, 12), row], self.rest[part])
            wait(z_in.at[k, pl.ds(0, 15), row], self.send_sem[part])
            flat = z_in.at[k].reshape(n * (params + 1) * 8, G)
            first, count = row.start, row.size

            def restage(owner, c):
                for i in range(8):
                    at = owner * (params + 1) * 8 + first * 8 + i
                    z[8 * owner + i, pl.ds(first, count)] = flat[pl.ds(at, count, stride=8), :]
                return c

            lax.fori_loop(0, n, restage, 0, unroll=4)

    colour_row = lax.broadcasted_iota(jnp.int32, (CP, 2 * G), 0) == params - 1
    colour_row = jnp.where(colour_row, 1.0, 0.0).astype(bf16)

    def transpose_rows(left, right_hi, right_lo, tinted):
        lh, ll = split2(left)
        first = dot(jnp.concatenate([lh, ll], axis=0), right_hi, NT)
        tinted = tinted[:, :G] + tinted[:, G:]
        last = dot(colour_row, jnp.concatenate(split2(tinted), axis=1), NT)
        return first[:CP] + first[CP:] + dot(lh, right_lo, NT) + last

    def pair(ref, t):
        return jnp.concatenate([ref[2 * t], ref[2 * t + 1]], axis=0)

    def diagonal(t, c):
        s, w = pair(S, t), pair(W, t)
        put_listing(t, transpose_rows(b16[t] * b16[t], *split2(s * s), w * w))
        return c

    lax.fori_loop(0, tiles, diagonal, 0, unroll=4)
    scatter_blocks(0)
    diag_sum = ViewScatter(0, 0)
    for part in range(2):
        diag_sum.start(part)
    render.publish(render.total())

    def apply_transpose(t, u):
        put_listing(t, transpose_rows(b16[t] * u, pair(hi, t), pair(lo, t), pair(W, t) * u))

    def gradient(t):
        u = lanes(u_now.at[0], 2 * t) - target[pl.ds(t, 1), :]
        residual[pl.ds(t, 1), :] = u
        apply_transpose(t, u)

    half_loop(mine, gradient, 8)
    for part in range(2):
        diag_sum.middle(part)
    render.rest()
    half_loop(other, gradient, 8)
    scatter_blocks(1)
    grad_sum = ViewScatter(1, 1)
    for part in range(2):
        grad_sum.start(part)

    R, P_, D = 0, 1, 2

    def lane_sum(x):
        return jnp.sum(x, axis=1, keepdims=True)

    def fold(x):
        return jnp.sum(jnp.sum(x, axis=0), axis=0, keepdims=True)

    for part in range(2):
        shard[D, rows_of(part)[2]] = diag_sum.total(part)
    for part in range(2):
        grad_sum.middle(part)

    def next_z(k, remainder):
        gather = ViewGather(k)
        inner = [jnp.zeros((1, G), f32)] * 3
        for part in range(2):
            row = rows_of(part)[2]
            r = remainder(part, row)
            shard[R, row] = r
            d = shard[D, row]
            zs = r / ((1.0 + DAMPING) * d + RIDGE)
            dz = (DAMPING * d + RIDGE) * zs
            inner = [inner[0] + fold(r * zs), inner[1] + fold(zs * dz), inner[2] + fold(shard[P_, row] * dz) if k else inner[2]]
            z_shard[k, row] = zs
            if part:
                z_shard[k, params] = jnp.concatenate(inner + [jnp.zeros((5, G), f32)], axis=0)
            gather.start(part)
        gather.relay(0)
        gather.relay(1)
        gather.finish(0)
        gather.finish(1)

    def share_square(k, u):
        squares = rows8(dot_in.at[k], 2 * view + core)
        squares[...] = jnp.broadcast_to(jnp.sum(u * u, axis=0, keepdims=True), (8, G))
        pair_sems = [new_sem(), new_sem()]

        def share(d, c):
            there = lax.rem(view + d, n)
            push(squares, squares, *pair_sems, (there, scene))
            push(squares, squares, *pair_sems, (there, scene + 1 - 2 * core))
            return c

        push(squares, squares, *pair_sems, partner)
        lax.fori_loop(1, n, share, 0)
        return pair_sems

    def all_squares(k, pair_sems):
        wait(dot_in.at[k, pl.ds(0, 8 * (2 * n - 1))], pair_sems[1])
        wait(dot_in.at[k, pl.ds(0, 8 * (2 * n - 1))], pair_sems[0])
        total = dot_in[k, pl.ds(0, 8), :]
        for i in range(1, 2 * n):
            total = total + dot_in[k, pl.ds(8 * i, 8), :]
        return lane_sum(total[0:1])

    one = jnp.ones((1, 1), f32)
    rz_old, pdp = one, 0.0 * one
    remainder = lambda part, row: -grad_sum.total(part)
    for k in range(ITERS):
        next_z(k, remainder)
        tally = z_in[k, 0, params]
        for i in range(1, n):
            tally = tally + z_in[k, i, params]
        tally_out[k] = tally
        tally_sems = [new_sem(), new_sem()]
        rows8(tally_in.at[k], scene)[...] = tally_out[k]
        to_scene(lambda peer: tally_out.at[k], rows8(tally_in.at[k], scene), *tally_sems)

        def forward(t):
            v = jnp.concatenate(
                [z[ids[j, t]] for j in range(2)], axis=1)
            vh, vl = split2(v)
            lhs = jnp.concatenate([vh, vl, vh], axis=0)
            total = jnp.zeros((1, 2 * G), f32)
            for j in range(2):
                p = 2 * t + j
                projected = dot(lhs[:, G * j : G * (j + 1)], bst[t], TN)
                tint = jnp.transpose(v[:, G * j : G * (j + 1)])[:, params - 1 : params]
                total = total + jnp.sum(S[p] * projected + W[p] * tint, axis=0, keepdims=True)
            put_u(t, total)

        product = SceneSum(k + 1)
        product.run(forward, 8)
        wait(some8(tally_in.at[k]), tally_sems[1])
        wait(some8(tally_in.at[k]), tally_sems[0])
        tally = tally_in[k, pl.ds(0, 8), :]
        for i in range(1, n):
            tally = tally + tally_in[k, pl.ds(8 * i, 8), :]
        totals = lane_sum(tally)
        rz, zdz, zdp = totals[0:1], totals[1:2], totals[2:3]
        beta = rz / rz_old if k else 0.0 * one
        u = product.total()
        if k:
            u = u + beta * half_rows(u_now.at[k], mine)[...]
        if k + 1 < ITERS:
            product.publish(u)
        pdp = zdz + 2.0 * beta * zdp + beta * beta * pdp
        pair_sems = share_square(k, u)
        if k:
            direction[...] = z[...] + beta * direction[...]
            shard[P_] = z_shard[k, pl.ds(0, params)] + beta * shard[P_]
        else:
            direction[...] = z[...]
            shard[P_] = z_shard[k, pl.ds(0, params)]
        if k + 1 < ITERS:
            back = lambda t: apply_transpose(t, lanes(u_now.at[k + 1], 2 * t))
            half_loop(mine, back, 8)
            product.rest()
            half_loop(other, back, 8)
            scatter_blocks(k)
            image_sum = ViewScatter(k + 2, k)
            image_sum.start(0)
            image_sum.start(1)
            a = rz / (all_squares(k, pair_sems) + pdp)
            image_sum.middle(0)
            image_sum.middle(1)

            def remainder(part, row, image_sum=image_sum, a=a):
                image = image_sum.total(part) + (DAMPING * shard[D, row] + RIDGE) * shard[P_, row]
                return shard[R, row] - a * image

            if k:
                total_step[...] = total_step[...] + a * direction[...]
            else:
                total_step[...] = a * direction[...]
        else:
            def put_step(b, c):
                at = pl.ds(pl.multiple_of(b * G, G), G)
                base[:, at] = total_step[b][:params]
                last_direction[:, at] = direction[b][:params]
                return c

            lax.fori_loop(0, G, put_step, 0, unroll=8)
            a = rz / (all_squares(k, pair_sems) + pdp)
            scale[...] = jnp.broadcast_to(a, scale.shape)
        rz_old = rz


def local(n, params, pixel_basis, tile_blocks, depth_rank, target):
    count = params.shape[0]
    tiles, _, pixels = pixel_basis.shape
    ids = tile_blocks.transpose(1, 2, 0).reshape(2, tiles)
    basis = pixel_basis.transpose(1, 0, 2).reshape((count - 1) * tiles, pixels)
    vmem = pl.BlockSpec(memory_space=pltpu.VMEM)
    lists = 2 * tiles
    base, direction, scale, residual = pl.pallas_call(
        functools.partial(kernel, n, count, tiles),
        out_shape=(
            jax.ShapeDtypeStruct((count, G * G), f32),
            jax.ShapeDtypeStruct((count, G * G), f32),
            jax.ShapeDtypeStruct((1, G * G), f32),
            jax.ShapeDtypeStruct((tiles, pixels), f32),
        ),
        in_specs=[vmem, vmem, pl.BlockSpec(memory_space=pltpu.SMEM), vmem, vmem, vmem],
        out_specs=(vmem,) * 4,
        scratch_shapes=[
            pltpu.VMEM((tiles, CP, pixels), f32),
            pltpu.VMEM((tiles, 3 * CP, pixels), bf16),
            pltpu.VMEM((lists, G, pixels), f32),
            pltpu.VMEM((lists, G, pixels), f32),
            pltpu.VMEM((lists, G, pixels), bf16),
            pltpu.VMEM((lists, G, pixels), bf16),
            pltpu.VMEM((CP * lists, G), f32),
            pltpu.VMEM((G, 2 * lists), bf16),
            pltpu.VMEM((8 * n, G), f32),
            pltpu.VMEM((8 * n, G), f32),
            pltpu.VMEM((8 * n, G), f32),
            pltpu.VMEM((8 * n, G), f32),
            pltpu.VMEM((2 * tiles, G), f32),
            pltpu.VMEM((ITERS + 1, tiles, G), f32),
            pltpu.VMEM((ITERS + 1, n // 2, tiles, G), f32),
            pltpu.VMEM((ITERS + 1, 2 * tiles, G), f32),
            pltpu.VMEM((ITERS, 8, G), f32),
            pltpu.VMEM((ITERS, 8 * n, G), f32),
            pltpu.VMEM((2, n, count, 8, G), f32),
            pltpu.VMEM((ITERS + 1, SIDE - 1, SIDE, count, 8, G), f32),
            pltpu.VMEM((ITERS + 1, SIDE, count, 8, G), f32),
            pltpu.VMEM((ITERS + 1, SIDE - 1, count, 8, G), f32),
            pltpu.VMEM((G, CP, G), f32),
            pltpu.VMEM((ITERS, n, count + 1, 8, G), f32),
            pltpu.VMEM((G, CP, G), f32),
            pltpu.VMEM((G, CP, G), f32),
            pltpu.VMEM((ITERS, count + 1, 8, G), f32),
            pltpu.VMEM((3, count, 8, G), f32),
            pltpu.VMEM((ITERS, 16 * n, G), f32),
            pltpu.SemaphoreType.DMA((SEMS,)),
        ],
        compiler_params=pltpu.CompilerParams(
            collective_id=0, has_side_effects=True, vmem_limit_bytes=64 * 1024 * 1024 - 65536),
        name="lm_step",
    )(params, basis, ids, ids, depth_rank, target)
    return base + scale * direction, residual


def solution(mesh):
    in_specs = (
        P(None, "scene"),
        P("view", None, None),
        P("view", "scene", None),
        P("view", None),
        P("view", None),
    )
    out_specs = (P(None, "scene"), P("view", None))
    step = functools.partial(local, mesh.shape["scene"])
    return jax.shard_map(step, mesh=mesh, in_specs=in_specs, out_specs=out_specs, check_vma=False)
```

time: 166 us -> 151 us (0.910)
  Pallas kernels: 162 us -> 147 us
  other arithmetic: 0 us -> 2.64 us
  local copies, waits for them, and re-layouts: 2.89 us -> 0.62 us
    pallas_call x1, Pallas kernels: 162 us -> 147 us  [local(): pl.pallas_call(functools.partial(kernel, n, count, tiles), out_shape=(jax...]
    add x0 -> x1, other arithmetic: none -> 2.64 us  [local(): return (base + scale * direction, residual)]
    unnamed x4 -> x3, local copies, waits for them, and re-layouts: 2.89 us -> 0.62 us
where the time goes in v3:
time: 151 us
  Pallas kernels  147 us (97%)
  other arithmetic  2.64 us (2%)
    pallas_call x1, Pallas kernels, local(): pl.pallas_call(functools.partial(kernel, n, count, tiles), out_shape=(jax...  147 us

profile of v3, /device:TPU:1, one launch (start us, length us, event | category | flops | bytes accessed | tf_op | source)
XLA Modules:
  0.0 150.9 jit_solution(15457309546934673590)
XLA Ops:
  0.6 146.9 %lm_step.1 = (f32[14,16384]{1,0:T(8,128)}, f32[14,16384]{1,0:T(8,128)}, f32[1,16384]{1,0:T(1,128)}, f32[32,256]{1,0:T(8,128)}) custom-call(f32[14,16384]{1,0:T(8,128)} %par.1, f32[416,256]{1,0:T(8,128)} %bitcast.7, s32[2,32]{1,0:T(2,128)} %bitcast.9, s32[2,32]{1,0:T(2,128)} %bitcast.10, s32[32,32]{1,0:T(8,128)} %rank.1, f32[32,256]{1,0:T(8,128)} %target.1), custom_call_target="tpu_custom_call" | custom-call | tf_op jit(solution)/shard_map/lm_step/pallas_call | solution.py:560
  147.6 0.0 copy-start
  147.6 2.6 %multiply_add_fusion = f32[14,16384]{1,0:T(8,128)} fusion(f32[14,16384]{1,0:T(8,128)} %get-tuple-element.6, f32[14,16384]{1,0:T(8,128)} %get-tuple-element.8, f32[16384]{0:T(1024)} %bitcast.8), kind=kLoop, calls=%fused_computation | loop fusion | flops 458752 | bytes 2818048 | tf_op jit(solution)/shard_map/add | solution.py:606
  150.2 0.0 copy-done
  150.2 0.6 copy.8
Async XLA Ops:
  147.6 2.7 %copy-start = (f32[32,256]{1,0:T(8,128)S(1)}, f32[32,256]{1,0:T(8,128)}, u32[]{:S(2)}) copy-start(f32[32,256]{1,0:T(8,128)} %get-tuple-element.13) | copy-start | bytes 98308

commit v4 on v3

--- a/solution.py
+++ b/solution.py
@@ -59,6 +59,8 @@
     y, x = view // SIDE, lax.rem(view, SIDE)
     zz, core = scene // 2, lax.rem(scene, 2)
     partner = (view, scene + 1 - 2 * core)
+    xs = [lax.rem(x + d, SIDE) for d in range(SIDE)]
+    ys = [lax.rem(y + d, SIDE) for d in range(SIDE)]
     barrier = pltpu.get_barrier_semaphore()
 
     def greet(d, c):
@@ -87,9 +89,6 @@
 
         lax.fori_loop(1, n, body, 0)
 
-    block_at = lax.broadcasted_iota(jnp.int32, (G, tiles), 0)
-    hot = [jnp.where(block_at == ids_rows[pl.ds(j, 1), :], 1.0, 0.0).astype(bf16) for j in range(2)]
-    onehot[...] = jnp.concatenate(hot + hot, axis=1)
     below = lax.broadcasted_iota(jnp.int32, (G, G), 1) < lax.broadcasted_iota(jnp.int32, (G, G), 0)
     below = jnp.where(below, 1.0, 0.0).astype(bf16)
     below = jnp.concatenate([below, below], axis=1)
@@ -102,8 +101,6 @@
         full = jnp.concatenate([half[pl.ds(t, params - 1, stride=tiles), :] for half in halves], axis=1)
         full = jnp.concatenate([full, jnp.zeros((CP - params + 1, full.shape[1]), f32)], axis=0)
         b16[t] = full
-        bh, bl = split2(full)
-        bst[t] = jnp.concatenate([bh, bh, bl], axis=0)
         return c
 
     lax.fori_loop(0, tiles, prepare, 0, unroll=4)
@@ -151,6 +148,17 @@
     to_scene(lambda peer: rows8(bl_out, peer), rows8(bl_in, scene), front_sems[0], front_sems[1])
     rows8(bl_in, scene)[...] = rows8(bl_out, scene)[...]
 
+    block_at = lax.broadcasted_iota(jnp.int32, (G, tiles), 0)
+    hot = [jnp.where(block_at == ids_rows[pl.ds(j, 1), :], 1.0, 0.0).astype(bf16) for j in range(2)]
+    onehot[...] = jnp.concatenate(hot + hot, axis=1)
+
+    def basis_halves(t, c):
+        bh, bl = split2(b16[t])
+        bst[t] = jnp.concatenate([bh, bh, bl], axis=0)
+        return c
+
+    lax.fori_loop(0, tiles, basis_halves, 0, unroll=4)
+
     def weights(t, c):
         for j in range(2):
             p = 2 * t + j
@@ -163,7 +171,7 @@
             S[p] = w * colour * (1.0 - o * (1.0 / ALPHA))
         return c
 
-    lax.fori_loop(0, tiles // 2, weights, 0, unroll=4)
+    lax.fori_loop(0, tiles // 4, weights, 0, unroll=4)
 
     wait(some8(bl_in), front_sems[1])
     wait(some8(bl_out), front_sems[0])
@@ -180,7 +188,7 @@
     to_scene(lambda peer: rows8(fr_out, peer), rows8(fr_in, scene), front_sems[2], front_sems[3])
     rows8(fr_in, scene)[...] = rows8(fr_out, scene)[...]
 
-    lax.fori_loop(tiles // 2, tiles, weights, 0, unroll=4)
+    lax.fori_loop(tiles // 4, tiles, weights, 0, unroll=4)
     wait(some8(fr_in), front_sems[3])
     wait(some8(fr_out), front_sems[2])
 
@@ -216,24 +224,39 @@
         end = end + more * part
         return pl.ds(a, b - a), pl.ds(b, end - b), pl.ds(a, end - a)
 
-    at_x = lambda d: (y * SIDE + lax.rem(x + d, SIDE), scene)
-    at_y = lambda d: (lax.rem(y + d, SIDE) * SIDE + x, scene)
+    row_to = [y * SIDE + xs[d] for d in range(SIDE)]
+    column_to = [ys[d] * SIDE + x for d in range(SIDE)]
+    at_x = lambda d: (row_to[d], scene)
+    at_y = lambda d: (column_to[d], scene)
 
     half_rows = lambda ref, first: ref.at[pl.ds(pl.multiple_of(2 * first, 8), tiles)]
 
     class SceneSum:
         def __init__(self, q):
-            self.q, self.sems = q, [new_sem() for _ in range(6)]
+            self.q, self.sems = q, [new_sem() for _ in range(7)]
 
         def run(self, body, unroll):
             q, sem = self.q, self.sems
-            half_loop(other, body, unroll)
-            push(half_rows(u_out, other), u_pair.at[q], sem[0], sem[1], partner)
-            half_loop(mine, body, unroll)
-            wait(u_pair.at[q], sem[1])
-            u_z[q, zz] = half_rows(u_out, mine)[...] + u_pair[q]
-            for d in (4, 3, 5, 2, 6, 1, 7):
-                push(u_z.at[q, zz], u_z.at[q, zz], sem[2], sem[3], (view, lax.rem(scene + 2 * d, n)))
+            quarter = tiles // 4
+
+            def part_loop(first):
+                def step_of(i, c):
+                    body(first + i)
+                    return c
+
+                lax.fori_loop(0, quarter, step_of, 0, unroll=unroll)
+
+            rows = lambda ref, first: ref.at[pl.ds(pl.multiple_of(2 * first, 8), 2 * quarter)]
+            for i in range(2):
+                part_loop(other + i * quarter)
+                push(rows(u_out, other + i * quarter), rows(u_pair.at[q], i * quarter), sem[0], sem[1 + 5 * i], partner)
+            for i in range(2):
+                part_loop(mine + i * quarter)
+                pair_rows, z_rows = rows(u_pair.at[q], i * quarter), rows(u_z.at[q, zz], i * quarter)
+                wait(pair_rows, sem[1 + 5 * i])
+                z_rows[...] = rows(u_out, mine + i * quarter)[...] + pair_rows[...]
+                for d in (4, 3, 5, 2, 6, 1, 7):
+                    push(z_rows, z_rows, sem[2], sem[3], (view, lax.rem(scene + 2 * d, n)))
             wait(u_pair.at[q], sem[0])
 
         def total(self):
@@ -283,28 +306,23 @@
             row_a, row_b, _ = rows_of(part)
             for e in (2, 1, 3, 0):
                 for d in (2, 1, 3):
-                    to_x, to_y = lax.rem(x + d, SIDE), lax.rem(y + d, SIDE)
-                    line_y, line_x = lax.rem(y + e, SIDE), lax.rem(x + e, SIDE)
+                    to_x, to_y, line_y, line_x = xs[d], ys[d], ys[e], xs[e]
                     push(w_out.at[slot, line_y * SIDE + to_x, row_a], parts.at[q, d - 1, line_y, row_a],
-                         self.send_sem[part], self.first[part][0][e], (y * SIDE + to_x, scene))
+                         self.send_sem[part], self.first[part][0][e], at_x(d))
                     push(w_out.at[slot, to_y * SIDE + line_x, row_b], parts.at[q, d - 1, line_x, row_b],
-                         self.send_sem[part], self.first[part][1][e], (to_y * SIDE + x, scene))
+                         self.send_sem[part], self.first[part][1][e], at_y(d))
 
         def middle(self, part):
             q, slot = self.q, self.slot
             row_a, row_b, _ = rows_of(part)
             for e in (2, 1, 3, 0):
-                line_y, line_x = lax.rem(y + e, SIDE), lax.rem(x + e, SIDE)
-                for own, line, row, way, to in (
-                    (line_y * SIDE + x, line_y, row_a, 0, line_y * SIDE + x),
-                    (y * SIDE + line_x, line_x, row_b, 1, y * SIDE + line_x),
-                ):
+                for own, line, row, way in ((column_to[e], ys[e], row_a, 0), (row_to[e], xs[e], row_b, 1)):
                     wait(parts.at[q, :, line, row], self.first[part][way][e])
                     total = w_out[slot, own, row] + parts[q, 0, line, row]
                     half[q, line, row] = total + parts[q, 1, line, row] + parts[q, 2, line, row]
                     if e:
                         push(half.at[q, line, row], last.at[q, e - 1, row],
-                             self.send_sem[part], self.last[part][way], (to, scene))
+                             self.send_sem[part], self.last[part][way], (own, scene))
 
         def total(self, part):
             q, slot = self.q, self.slot
@@ -342,8 +360,7 @@
             row_a, row_b, _ = rows_of(part, 1)
             send_sem, rest = self.send_sem[part], self.rest[part]
             for d in (1, 3, 2):
-                from_x = y * SIDE + lax.rem(x + SIDE - d, SIDE)
-                from_y = lax.rem(y + SIDE - d, SIDE) * SIDE + x
+                from_x, from_y = row_to[SIDE - d], column_to[SIDE - d]
                 there_a, there_b = z_in.at[k, from_x, row_a], z_in.at[k, from_y, row_b]
                 wait(there_a, self.near[part][0][d - 1])
                 for e in (2, 1, 3):
@@ -402,14 +419,16 @@
         apply_transpose(t, u)
 
     half_loop(mine, gradient, 8)
-    for part in range(2):
-        diag_sum.middle(part)
     render.rest()
     half_loop(other, gradient, 8)
     scatter_blocks(1)
     grad_sum = ViewScatter(1, 1)
     for part in range(2):
         grad_sum.start(part)
+    for part in range(2):
+        diag_sum.middle(part)
+    for part in range(2):
+        grad_sum.middle(part)
 
     R, P_, D = 0, 1, 2
 
@@ -421,8 +440,6 @@
 
     for part in range(2):
         shard[D, rows_of(part)[2]] = diag_sum.total(part)
-    for part in range(2):
-        grad_sum.middle(part)
 
     def next_z(k, remainder):
         gather = ViewGather(k)
@@ -510,12 +527,14 @@
             product.publish(u)
         pdp = zdz + 2.0 * beta * zdp + beta * beta * pdp
         pair_sems = share_square(k, u)
-        if k:
-            direction[...] = z[...] + beta * direction[...]
-            shard[P_] = z_shard[k, pl.ds(0, params)] + beta * shard[P_]
-        else:
-            direction[...] = z[...]
-            shard[P_] = z_shard[k, pl.ds(0, params)]
+        def turn(k=k, beta=beta):
+            if k:
+                direction[...] = z[...] + beta * direction[...]
+                shard[P_] = z_shard[k, pl.ds(0, params)] + beta * shard[P_]
+            else:
+                direction[...] = z[...]
+                shard[P_] = z_shard[k, pl.ds(0, params)]
+
         if k + 1 < ITERS:
             back = lambda t: apply_transpose(t, lanes(u_now.at[k + 1], 2 * t))
             half_loop(mine, back, 8)
@@ -525,6 +544,7 @@
             image_sum = ViewScatter(k + 2, k)
             image_sum.start(0)
             image_sum.start(1)
+            turn()
             a = rz / (all_squares(k, pair_sems) + pdp)
             image_sum.middle(0)
             image_sum.middle(1)
@@ -538,6 +558,8 @@
             else:
                 total_step[...] = a * direction[...]
         else:
+            turn()
+
             def put_step(b, c):
                 at = pl.ds(pl.multiple_of(b * G, G), G)
                 base[:, at] = total_step[b][:params]

time: 151 us -> 147 us (0.974)
  Pallas kernels: 147 us -> 143 us
    pallas_call x1, Pallas kernels: 147 us -> 143 us  [local(): pl.pallas_call(functools.partial(kernel, n, count, tiles), out_shape=(jax...]
where the time goes in v4:
time: 147 us
  Pallas kernels  143 us (97%)
  other arithmetic  2.64 us (2%)
    pallas_call x1, Pallas kernels, local(): pl.pallas_call(functools.partial(kernel, n, count, tiles), out_shape=(jax...  143 us

profile of v4, /device:TPU:1, one launch (start us, length us, event | category | flops | bytes accessed | tf_op | source)
XLA Modules:
  0.0 146.9 jit_solution(6294258988081030525)
XLA Ops:
  0.6 143.0 %lm_step.1 = (f32[14,16384]{1,0:T(8,128)}, f32[14,16384]{1,0:T(8,128)}, f32[1,16384]{1,0:T(1,128)}, f32[32,256]{1,0:T(8,128)}) custom-call(f32[14,16384]{1,0:T(8,128)} %par.1, f32[416,256]{1,0:T(8,128)} %bitcast.7, s32[2,32]{1,0:T(2,128)} %bitcast.9, s32[2,32]{1,0:T(2,128)} %bitcast.10, s32[32,32]{1,0:T(8,128)} %rank.1, f32[32,256]{1,0:T(8,128)} %target.1), custom_call_target="tpu_custom_call" | custom-call | tf_op jit(solution)/shard_map/lm_step/pallas_call | solution.py:582
  143.6 0.0 copy-start
  143.6 2.6 %multiply_add_fusion = f32[14,16384]{1,0:T(8,128)} fusion(f32[14,16384]{1,0:T(8,128)} %get-tuple-element.6, f32[14,16384]{1,0:T(8,128)} %get-tuple-element.8, f32[16384]{0:T(1024)} %bitcast.8), kind=kLoop, calls=%fused_computation | loop fusion | flops 458752 | bytes 2818048 | tf_op jit(solution)/shard_map/add | solution.py:628
  146.3 0.0 copy-done
  146.3 0.6 copy.8
Async XLA Ops:
  143.6 2.7 %copy-start = (f32[32,256]{1,0:T(8,128)S(1)}, f32[32,256]{1,0:T(8,128)}, u32[]{:S(2)}) copy-start(f32[32,256]{1,0:T(8,128)} %get-tuple-element.13) | copy-start | bytes 98308

commit v5 on v4

--- a/solution.py
+++ b/solution.py
@@ -127,7 +127,7 @@
             vh, vm, vl = split3(listing_params(t, j))
             lhs = jnp.concatenate([vh, vh, vm, vh, vl, vm], axis=0)
             logit = dot(lhs, rhs, TN)
-            o = ALPHA * (1.0 / (1.0 + jnp.exp(-logit)))
+            o = 0.5 * ALPHA + 0.5 * ALPHA * jnp.tanh(0.5 * logit)
             keep = -o * (1.0 + o * (0.5 + o * (1.0 / 3.0 + o * 0.25)))
             W[p] = o
             kh, kl = split2(keep)
@@ -139,7 +139,7 @@
             bl_out[pl.ds(r + 1, 1), :] = total[:, G:]
         return c
 
-    lax.fori_loop(0, tiles, opacities, 0, unroll=4)
+    lax.fori_loop(0, tiles, opacities, 0, unroll=8)
 
     pl.semaphore_wait(barrier, 3 * (n - 1))
     rows8 = lambda ref, i: ref.at[pl.ds(pl.multiple_of(i * 8, 8), 8)]
@@ -171,7 +171,7 @@
             S[p] = w * colour * (1.0 - o * (1.0 / ALPHA))
         return c
 
-    lax.fori_loop(0, tiles // 4, weights, 0, unroll=4)
+    lax.fori_loop(0, tiles // 4, weights, 0, unroll=8)
 
     wait(some8(bl_in), front_sems[1])
     wait(some8(bl_out), front_sems[0])
@@ -188,7 +188,7 @@
     to_scene(lambda peer: rows8(fr_out, peer), rows8(fr_in, scene), front_sems[2], front_sems[3])
     rows8(fr_in, scene)[...] = rows8(fr_out, scene)[...]
 
-    lax.fori_loop(tiles // 4, tiles, weights, 0, unroll=4)
+    lax.fori_loop(tiles // 4, tiles, weights, 0, unroll=8)
     wait(some8(fr_in), front_sems[3])
     wait(some8(fr_out), front_sems[2])
 

time: 147 us -> 146 us (level)
  no operation moved by 1% of the time
where the time goes in v5:
time: 146 us
  Pallas kernels  142 us (97%)
  other arithmetic  2.64 us (2%)
    pallas_call x1, Pallas kernels, local(): pl.pallas_call(functools.partial(kernel, n, count, tiles), out_shape=(jax...  142 us

profile of v5, /device:TPU:1, one launch (start us, length us, event | category | flops | bytes accessed | tf_op | source)
XLA Modules:
  0.0 145.9 jit_solution(1813477058985398999)
XLA Ops:
  0.6 142.0 %lm_step.1 = (f32[14,16384]{1,0:T(8,128)}, f32[14,16384]{1,0:T(8,128)}, f32[1,16384]{1,0:T(1,128)}, f32[32,256]{1,0:T(8,128)}) custom-call(f32[14,16384]{1,0:T(8,128)} %par.1, f32[416,256]{1,0:T(8,128)} %bitcast.7, s32[2,32]{1,0:T(2,128)} %bitcast.9, s32[2,32]{1,0:T(2,128)} %bitcast.10, s32[32,32]{1,0:T(8,128)} %rank.1, f32[32,256]{1,0:T(8,128)} %target.1), custom_call_target="tpu_custom_call" | custom-call | tf_op jit(solution)/shard_map/lm_step/pallas_call | solution.py:582
  142.6 0.0 copy-start
  142.6 2.6 %multiply_add_fusion = f32[14,16384]{1,0:T(8,128)} fusion(f32[14,16384]{1,0:T(8,128)} %get-tuple-element.6, f32[14,16384]{1,0:T(8,128)} %get-tuple-element.8, f32[16384]{0:T(1024)} %bitcast.8), kind=kLoop, calls=%fused_computation | loop fusion | flops 458752 | bytes 2818048 | tf_op jit(solution)/shard_map/add | solution.py:628
  145.3 0.0 copy-done
  145.3 0.6 copy.8
Async XLA Ops:
  142.6 2.7 %copy-start = (f32[32,256]{1,0:T(8,128)S(1)}, f32[32,256]{1,0:T(8,128)}, u32[]{:S(2)}) copy-start(f32[32,256]{1,0:T(8,128)} %get-tuple-element.13) | copy-start | bytes 98308
